TPU v7x, 32 devices: a whole 2x2x4 slice. The times are simulated.
32 devices in a mesh: ctx: 8 (over y, x, core), head: 4 (over z).
Axes of the slice: x: 2, y: 2, z: 4, core: 2. Of those that a mesh axis runs over, the one named last changes fastest.
Arguments:
- head_inputs: bfloat16 [8192, 8192], P(('ctx', 'head')), may hold values from -6 to 6
- gate_inputs: bfloat16 [8192, 8192], P(('ctx', 'head')), may hold values from -6 to 6
- write_keys: bfloat16 [8192, 1024], P(('ctx', 'head')), may hold values from -6 to 6
- read_queries: bfloat16 [8192, 1024], P(('ctx', 'head')), may hold values from -0.5 to 0.5
- step_logits: bfloat16 [8192, 128], P(('ctx', 'head')), may hold values from -3 to 3
- step_bias: float32 [128], P('head'), may hold values from -6 to 0
- decay_log: float32 [128], P('head'), may hold values from -7 to -2
- skip_scale: float32 [128], P('head'), may hold values from 0.5 to 1.5
- norm_gain: float32 [8192], replicated, may hold values from 0.1 to 1.9
- document_starts: int32 [32], P('ctx'), may hold values from 0 to 256, as said below
Outputs:
- layer_output: bfloat16 [8192, 8192], P(('ctx', 'head'))
Inputs may be any that keep to these rules, and one draw needn't show every extreme that they name: `document_starts`: each entry is the position within its block of 256 tokens at which a document starts, or 256 where none starts; the first block starts one at 0.
All inputs are finite; a program needn't handle non-finite values.
Results may differ from a plain program's by a relative error of at most 0.0058.
Values may be sent and summed in bfloat16 or wider, within the bound.
A program may use at most 128 MiB of HBM per device.

v0:
```python
import functools

import jax
import jax.numpy as jnp
from jax import lax
from jax.experimental import pallas as pl
from jax.experimental.pallas import tpu as pltpu
from jax.sharding import PartitionSpec as P

HEAD_DIM = 64
STATE = 128
BLOCK = 256
CHUNK = 256
SKEW = 3
EARLY = 2
ROWS = 32
MESH = pl.DeviceIdType.MESH
F32 = jnp.float32
BF16 = jnp.bfloat16


def split_terms(value, terms):
    parts = []
    for _ in range(terms):
        part = value.astype(BF16)
        parts.append(part)
        value = value - part.astype(F32)
    return parts


def spread_matrix(heads, first_head, width):
    row = lax.broadcasted_iota(jnp.int32, (2 * heads, width), 0)
    lane = lax.broadcasted_iota(jnp.int32, (2 * heads, width), 1)
    own = lane // HEAD_DIM + first_head
    return jnp.where((row == own) | (row == own + heads), 1.0, 0.0).astype(BF16)


def exchange_kernel(
    n, m, groups,
    x_hbm, b_hbm, c_hbm, logit_hbm, bias_hbm, decay_hbm, skip_hbm, starts_hbm,
    mixed_hbm,
    x_ref, b_ref, c_ref, logit_ref, bias_ref, decay_ref, skip_ref, starts_ref, scores_ref, mixed_ref, param_ref,
    tail_ref, up_ref, down_ref, wide_ref, own_ref, sum_ref, before_ref,
    step_send, step_recv, fore_send, fore_recv, back_send, back_recv,
    param_in, decay_out, decay_in, hop_out, hop_in,
    param_sems, decay_sems, hop_sems, step_sems, fore_sems, back_sems, load_sems, mixed_sems,
):
    ci = lax.axis_index("ctx")
    zi = lax.axis_index("head")
    bits = m.bit_length() - 1
    length, inner = x_ref.shape
    heads = logit_ref.shape[1]
    count = inner // CHUNK
    per_group = count // groups
    chunk_heads = CHUNK // HEAD_DIM

    pairs = (
        (bias_hbm, bias_ref), (decay_hbm, decay_ref), (skip_hbm, skip_ref), (starts_hbm, starts_ref),
        (b_hbm, b_ref), (c_hbm, c_ref), (logit_hbm, logit_ref), (x_hbm, x_ref),
    )
    loads = [pltpu.make_async_copy(src, dst, load_sems.at[i]) for i, (src, dst) in enumerate(pairs)]
    for load in loads:
        load.start()

    def ctx_partner(j):
        bit = 1 << j
        upper = lax.rem(ci // bit, 2)
        return ci + bit - 2 * bit * upper, upper

    barrier = pltpu.get_barrier_semaphore()
    for d in range(1, n):
        pl.semaphore_signal(barrier, inc=1, device_id=(ci, lax.rem(zi + d, n)), device_id_type=MESH)
    for j in range(bits):
        pl.semaphore_signal(barrier, inc=1, device_id=(ctx_partner(j)[0], zi), device_id_type=MESH)

    own_heads = bias_ref.shape[1]
    place = jnp.where(
        lax.broadcasted_iota(jnp.int32, (own_heads, heads), 0) + zi * own_heads
        == lax.broadcasted_iota(jnp.int32, (own_heads, heads), 1), 1.0, 0.0
    ).astype(BF16)
    for load in loads[:4]:
        load.wait()
    raw = jnp.concatenate(
        [bias_ref[...], decay_ref[...], skip_ref[...], jnp.zeros((5, own_heads), F32)], axis=0
    )
    placed = jnp.zeros((8, heads), F32)
    for part in split_terms(raw, 3):
        placed = placed + jnp.dot(part, place, preferred_element_type=F32)
    param_ref[...] = placed
    pl.semaphore_wait(barrier, n - 1 + bits)

    def remote(src, dst, sems, index, device):
        return pltpu.make_async_remote_copy(
            src_ref=src, dst_ref=dst, send_sem=sems.at[(0, *index)], recv_sem=sems.at[(1, *index)],
            device_id=device, device_id_type=MESH,
        )

    def peer(d):
        return (ci, lax.rem(zi + d, n))

    param_copies = [
        remote(param_ref, param_in.at[d], param_sems, (d,), peer(d)) for d in range(1, n)
    ]
    for copy in param_copies:
        copy.start()

    offset = lax.rem(zi * length, BLOCK)
    starts = starts_ref[...].astype(F32)
    mine = lax.broadcasted_iota(jnp.int32, starts.shape, 1) == zi * length // BLOCK
    start = jnp.sum(jnp.where(mine, starts, 0.0), axis=1, keepdims=True) - offset.astype(F32)
    start = jnp.where((start < 0.0) | (start >= length), float(length), start)
    row = lax.broadcasted_iota(jnp.int32, (length, length), 0).astype(F32)
    col = lax.broadcasted_iota(jnp.int32, (length, length), 1).astype(F32)
    lower = jnp.where(row >= col, 1.0, 0.0)
    same = jnp.where(row >= start, 1.0, 0.0) == jnp.where(col >= start, 1.0, 0.0)
    allowed = jnp.where(same, lower, 0.0)
    for load in loads[4:7]:
        load.wait()
    for g in range(groups):
        part = slice(g * STATE, (g + 1) * STATE)
        scores = lax.dot_general(
            c_ref[:, part], b_ref[:, part], (((1,), (1,)), ((), ())), preferred_element_type=F32
        )
        scores_ref[g] = jnp.where(allowed > 0.0, scores, 0.0).astype(BF16)

    for copy in param_copies:
        copy.wait()
    params = param_ref[...]
    for d in range(1, n):
        params = params + param_in[d]

    logits = logit_ref[...].astype(F32) + params[0:1]
    step = jnp.maximum(logits, 0.0) + jnp.log1p(jnp.exp(-jnp.abs(logits)))
    rate = -jnp.exp(params[1:2]) * step
    lower = lower.astype(BF16)
    cum = jnp.zeros((length, heads), F32)
    for part in split_terms(rate, 3)[::-1]:
        cum = cum + jnp.dot(lower, part, preferred_element_type=F32)
    last = cum[length - 1 : length]
    middle = cum[length // 2 - 1 : length // 2]
    position = lax.broadcasted_iota(jnp.int32, (length, heads), 0).astype(F32)
    begins = start < length
    carried = jnp.where(begins, 0.0, jnp.exp(last))

    decay_out[...] = jnp.broadcast_to(carried, decay_out.shape)
    decay_copies = [
        remote(decay_out, decay_in.at[d], decay_sems, (d,), peer(d)) for d in range(1, n)
    ]
    for copy in decay_copies:
        copy.start()
    keep = position >= jnp.where(begins, start, 0.0)
    tail = jnp.where(keep, jnp.exp(last - cum), 0.0) * step
    tail_ref[...] = jnp.concatenate(split_terms(tail, 2), axis=1)
    up_ref[...] = jnp.concatenate(split_terms(jnp.exp(cum - middle), 2), axis=1)
    down_ref[...] = jnp.concatenate(split_terms(jnp.exp(middle - cum) * step, 2), axis=1)
    loads[7].wait()
    for copy in decay_copies:
        copy.wait()
    before = jnp.ones((8, heads), F32)
    after = jnp.ones((8, heads), F32)
    for d in range(1, n):
        got = decay_in[d]
        before = before * jnp.where(zi >= d, got, 1.0)
        after = after * jnp.where(zi >= d, 1.0, got)
    own = jnp.broadcast_to(carried, (8, heads))
    total = before * own * after
    ahead = jnp.ones((8, heads), F32)
    after_parts = jnp.concatenate(split_terms(after, 2), axis=1)

    def step_copy(j, k):
        return remote(step_send.at[j, k], step_recv.at[j, k], step_sems, (j, k), (ctx_partner(j)[0], zi))

    def fore_copy(k):
        return remote(fore_send.at[k], fore_recv.at[k], fore_sems, (k,), (ci, lax.rem(zi + 1, n)))

    def back_copy(k):
        return remote(back_send.at[k], back_recv.at[k], back_sems, (k,), (ci, lax.rem(zi + n - 1, n)))

    def store_copy(k):
        channels = pl.ds(pl.multiple_of(k * CHUNK, CHUNK), CHUNK)
        return pltpu.make_async_copy(mixed_ref.at[k], mixed_hbm.at[:, channels], mixed_sems.at[k])

    def line(k, slot):
        return wide_ref[k, slot : slot + 1, :]

    is_last_upper = ctx_partner(bits - 1)[1] == 1
    is_last_lower = ctx_partner(bits - 1)[1] == 0

    def write(k, _):
        matrix = spread_matrix(heads, k * chunk_heads, CHUNK)
        weight = jnp.dot(tail_ref[...], matrix, preferred_element_type=F32)
        scale = jnp.dot(after_parts, matrix, preferred_element_type=F32)[0:1]
        channels = pl.ds(pl.multiple_of(k * CHUNK, CHUNK), CHUNK)
        scaled = (x_ref[:, channels].astype(F32) * weight).astype(BF16)
        keys = b_ref[:, pl.ds(pl.multiple_of((k // per_group) * STATE, STATE), STATE)]
        written = lax.dot_general(keys, scaled, (((0,), (0,)), ((), ())), preferred_element_type=F32)
        own_ref[k] = written
        value = written * scale
        sum_ref[k] = value
        step_send[0, k] = value.astype(BF16)
        step_copy(0, k).start()
        return 0

    middle_factor = jnp.broadcast_to(jnp.exp(middle), (8, heads))
    coefs = [middle_factor, jnp.broadcast_to(params[2:3], (8, heads)), own, before]
    for j in range(bits):
        partner, upper = ctx_partner(j)
        hop_out[j] = total
        copy = remote(hop_out.at[j], hop_in.at[j], hop_sems, (j,), (partner, zi))
        copy.start()
        lax.fori_loop(j * EARLY, (j + 1) * EARLY, write, 0)
        copy.wait()
        got = hop_in[j]
        is_upper = upper == 1
        coefs.append(jnp.where(is_upper, 1.0, got))
        coefs.append(jnp.where(is_upper, total, 1.0))
        coefs.append(jnp.where(is_upper, ahead, 0.0))
        ahead = jnp.where(is_upper, ahead * got, ahead)
        total = total * got
    slots = wide_ref.shape[1]
    pad = [jnp.zeros((1, heads), F32)] * (slots - len(coefs))
    table = jnp.concatenate([c[0:1] for c in coefs] + pad, axis=0)
    table = jnp.concatenate(split_terms(table, 2), axis=1)

    fore_at = (bits - 1 + zi) * SKEW
    back_at = (bits - 1 + n - 1 - zi) * SKEW
    done_at = jnp.maximum(fore_at, back_at)

    def iteration(t, _):
        kw = t + bits * EARLY

        @pl.when(kw < count)
        def _():
            write(kw, 0)

        for j in range(bits):
            k = t - j * SKEW

            @pl.when((k >= 0) & (k < count))
            def _(j=j, k=k):
                if j == 0:
                    matrix = spread_matrix(heads, k * chunk_heads, CHUNK)
                    wide_ref[k] = jnp.dot(table, matrix, preferred_element_type=F32)
                    before_ref[k] = jnp.zeros_like(before_ref[k])

                def receive():
                    step_copy(j, k).wait_recv()
                    got = step_recv[j, k].astype(F32)
                    before_ref[k] += line(k, 6 + 3 * j) * got
                    return got

                if j == bits - 1:
                    @pl.when(is_last_upper)
                    def _():
                        receive()

                else:
                    got = receive()
                    value = sum_ref[k] * line(k, 4 + 3 * j) + line(k, 5 + 3 * j) * got
                    sum_ref[k] = value

                    def send():
                        step_send[j + 1, k] = value.astype(BF16)
                        step_copy(j + 1, k).start()

                    if j == bits - 2:
                        pl.when(is_last_lower)(send)
                    else:
                        send()

        kf = t - fore_at

        @pl.when((kf >= 0) & (kf < count))
        def _():
            @pl.when(zi > 0)
            def _():
                fore_copy(kf).wait_recv()

            @pl.when(zi == 0)
            def _():
                fore_recv[kf] = jnp.zeros_like(fore_recv[kf])

            @pl.when(zi < n - 1)
            def _():
                arrived = fore_recv[kf].astype(F32) + line(kf, 3) * before_ref[kf]
                fore_send[kf] = (line(kf, 2) * arrived + own_ref[kf]).astype(BF16)
                fore_copy(kf).start()

        kb = t - back_at

        @pl.when((kb >= 0) & (kb < count))
        def _():
            @pl.when(zi < n - 1)
            def _():
                back_copy(kb).wait_recv()

            @pl.when(zi == n - 1)
            def _():
                back_recv[kb] = jnp.zeros_like(back_recv[kb])

            @pl.when(zi > 0)
            def _():
                back_send[kb] = (back_recv[kb].astype(F32) + before_ref[kb]).astype(BF16)
                back_copy(kb).start()

        kd = t - done_at

        @pl.when((kd >= 0) & (kd < count))
        def _():
            incoming = before_ref[kd] + back_recv[kd].astype(F32)
            frozen = (fore_recv[kd].astype(F32) + line(kd, 3) * incoming).astype(BF16)
            matrix = spread_matrix(heads, kd * chunk_heads, CHUNK)
            up = jnp.dot(up_ref[...], matrix, preferred_element_type=F32)
            down = jnp.dot(down_ref[...], matrix, preferred_element_type=F32)
            x = x_ref[:, pl.ds(pl.multiple_of(kd * CHUNK, CHUNK), CHUNK)].astype(F32)
            group = kd // per_group
            inside = jnp.dot(scores_ref[group], (x * down).astype(BF16), preferred_element_type=F32)
            queries = c_ref[:, pl.ds(pl.multiple_of(group * STATE, STATE), STATE)]
            outside = jnp.dot(queries, frozen, preferred_element_type=F32)
            place_in = lax.broadcasted_iota(jnp.int32, outside.shape, 0).astype(F32)
            outside = jnp.where(place_in < start, outside * line(kd, 0), 0.0)
            mixed_ref[kd] = (up * (inside + outside) + line(kd, 1) * x).astype(BF16)
            store_copy(kd).start()

        return 0

    lax.fori_loop(0, count + (bits - 1 + n - 1) * SKEW, iteration, 0)

    def drain(k, _):
        for j in range(bits - 1):
            step_copy(j, k).wait_send()

        @pl.when(is_last_lower)
        def _():
            step_copy(bits - 1, k).wait_send()

        @pl.when(zi < n - 1)
        def _():
            fore_copy(k).wait_send()

        @pl.when(zi > 0)
        def _():
            back_copy(k).wait_send()

        store_copy(k).wait()
        return 0

    lax.fori_loop(0, count, drain, 0)


def norm_kernel(mixed_ref, gate_ref, gain_ref, out_ref, gated_ref):
    rows, inner = mixed_ref.shape
    width = 1024
    power = jnp.zeros((rows, 1), F32)
    for i in range(inner // width):
        channels = slice(i * width, (i + 1) * width)
        gate = gate_ref[:, channels].astype(F32)
        gated = mixed_ref[:, channels].astype(F32) * (gate / (1.0 + jnp.exp(-gate)))
        gated_ref[:, channels] = gated
        power = power + jnp.sum(gated * gated, axis=1, keepdims=True)
    factor = lax.rsqrt(power / inner + 1e-05)
    for i in range(inner // width):
        channels = slice(i * width, (i + 1) * width)
        out_ref[:, channels] = (gated_ref[:, channels] * factor * gain_ref[:, channels]).astype(BF16)


def local(
    n, m,
    head_inputs, gate_inputs, write_keys, read_queries, step_logits,
    step_bias, decay_log, skip_scale, norm_gain, document_starts,
):
    length, inner = head_inputs.shape
    heads = step_logits.shape[1]
    groups = write_keys.shape[1] // STATE
    assert length <= BLOCK and BLOCK % length == 0 and m & (m - 1) == 0 and m > 1
    bits = m.bit_length() - 1
    count = inner // CHUNK

    slots = 24
    assert bits * EARLY <= count and 4 + 3 * bits <= slots
    hbm = pl.BlockSpec(memory_space=pltpu.HBM)
    anywhere = pl.BlockSpec(memory_space=pl.ANY)
    piece = (count, STATE, CHUNK)
    dma = pltpu.SemaphoreType.DMA
    mixed = pl.pallas_call(
        functools.partial(exchange_kernel, n, m, groups),
        out_shape=jax.ShapeDtypeStruct((length, inner), BF16),
        in_specs=[hbm] * 8,
        out_specs=anywhere,
        scratch_shapes=[
            pltpu.VMEM((length, inner), BF16),
            pltpu.VMEM(write_keys.shape, BF16),
            pltpu.VMEM(read_queries.shape, BF16),
            pltpu.VMEM(step_logits.shape, BF16),
            pltpu.VMEM((1, step_bias.shape[0]), F32),
            pltpu.VMEM((1, step_bias.shape[0]), F32),
            pltpu.VMEM((1, step_bias.shape[0]), F32),
            pltpu.VMEM((1, document_starts.shape[0]), jnp.int32),
            pltpu.VMEM((groups, length, length), BF16),
            pltpu.VMEM((count, length, CHUNK), BF16),
            pltpu.VMEM((8, heads), F32),
            pltpu.VMEM((length, 2 * heads), BF16),
            pltpu.VMEM((length, 2 * heads), BF16),
            pltpu.VMEM((length, 2 * heads), BF16),
            pltpu.VMEM((count, slots, CHUNK), F32),
            pltpu.VMEM(piece, F32),
            pltpu.VMEM(piece, F32),
            pltpu.VMEM(piece, F32),
            pltpu.VMEM((bits, *piece), BF16),
            pltpu.VMEM((bits, *piece), BF16),
            pltpu.VMEM(piece, BF16),
            pltpu.VMEM(piece, BF16),
            pltpu.VMEM(piece, BF16),
            pltpu.VMEM(piece, BF16),
            pltpu.VMEM((n, 8, heads), F32),
            pltpu.VMEM((8, heads), F32),
            pltpu.VMEM((n, 8, heads), F32),
            pltpu.VMEM((bits, 8, heads), F32),
            pltpu.VMEM((bits, 8, heads), F32),
            dma((2, n)),
            dma((2, n)),
            dma((2, bits)),
            dma((2, bits, count)),
            dma((2, count)),
            dma((2, count)),
            dma((8,)),
            dma((count,)),
        ],
        compiler_params=pltpu.CompilerParams(
            collective_id=0, has_side_effects=True, vmem_limit_bytes=56 * 2**20
        ),
        name="exchange",
    )(
        head_inputs, write_keys, read_queries, step_logits,
        step_bias[None], decay_log[None], skip_scale[None], document_starts[None],
    )

    tile = min(length, ROWS)
    tokens = pl.BlockSpec((tile, inner), lambda i: (i, 0))
    return pl.pallas_call(
        norm_kernel,
        grid=(length // tile,),
        out_shape=jax.ShapeDtypeStruct((length, inner), BF16),
        in_specs=[tokens, tokens, pl.BlockSpec((1, inner), lambda i: (0, 0))],
        out_specs=tokens,
        scratch_shapes=[pltpu.VMEM((tile, inner), F32)],
        compiler_params=pltpu.CompilerParams(vmem_limit_bytes=20 * 2**20),
        name="norm",
    )(mixed, gate_inputs, norm_gain[None])


def solution(mesh):
    tokens = P(("ctx", "head"), None)
    return jax.shard_map(
        functools.partial(local, mesh.shape["head"], mesh.shape["ctx"]),
        mesh=mesh,
        in_specs=(tokens,) * 5 + (P("head"), P("head"), P("head"), P(), P("ctx")),
        out_specs=tokens,
        check_vma=False,
    )
```

profile of v0, /device:TPU:0, one launch (start us, length us, event | category | flops | bytes accessed | tf_op | source)
XLA Modules:
  0.0 94.2 jit_solution(9276936966697916038)
XLA Ops:
  0.0 0.0 copy-start.1
  0.0 0.0 copy-start.2
  0.0 85.6 %exchange.1.mixed_ref = bf16[256,8192]{1,0:T(8,128)(2,1)} custom-call(bf16[256,8192]{1,0:T(8,128)(2,1)} %x_hbm.1, bf16[256,1024]{1,0:T(8,128)(2,1)} %b_hbm.1, bf16[256,1024]{1,0:T(8,128)(2,1)} %c_hbm.1, bf16[256,128]{1,0:T(8,128)(2,1)} %logit_hbm.1, f32[1,32]{1,0:T(1,128)} %bitcast.6, f32[1,32]{1,0:T(1,128)} %bitcast.7, f32[1,32]{1,0:T(1,128)} %bitcast.8, ...), custom_call_target="tpu_custom_call" | custom-call | tf_op jit(solution)/shard_map/exchange/pallas_call | solution.py:385
  85.6 0.0 copy-done.1
  85.6 0.0 copy-done.2
  85.6 0.0 copy-start
  85.7 2.2 %copy-done = bf16[256,8192]{1,0:T(8,128)(2,1)S(1)} copy-done((bf16[256,8192]{1,0:T(8,128)(2,1)S(1)}, bf16[256,8192]{1,0:T(8,128)(2,1)}, u32[]{:S(2)}) %copy-start) | copy-done | bytes 4194328
  87.8 6.3 %norm.1 = bf16[256,8192]{1,0:T(8,128)(2,1)} custom-call(bf16[256,8192]{1,0:T(8,128)(2,1)S(1)} %copy-done, bf16[256,8192]{1,0:T(8,128)(2,1)S(1)} %copy-done.1, f32[1,8192]{1,0:T(1,128)S(1)} %bitcast.5), custom_call_target="tpu_custom_call" | custom-call | tf_op jit(solution)/shard_map/norm/pallas_call | solution.py:440
Async XLA Ops:
  0.0 85.6 %copy-start.1 = (bf16[256,8192]{1,0:T(8,128)(2,1)S(1)}, bf16[256,8192]{1,0:T(8,128)(2,1)}, u32[]{:S(2)}) copy-start(bf16[256,8192]{1,0:T(8,128)(2,1)} %gate_ref.1) | copy-start | bytes 12582916
  0.0 85.6 %copy-start.2 = (f32[8192]{0:T(1024)S(1)}, f32[8192]{0:T(1024)}, u32[]{:S(2)}) copy-start(f32[8192]{0:T(1024)} %param.18) | copy-start | bytes 98308
  85.6 2.2 %copy-start = (bf16[256,8192]{1,0:T(8,128)(2,1)S(1)}, bf16[256,8192]{1,0:T(8,128)(2,1)}, u32[]{:S(2)}) copy-start(bf16[256,8192]{1,0:T(8,128)(2,1)} %exchange.1.mixed_ref) | copy-start | bytes 12582916
where the time goes:
time: 94.3 us; the launch traced here: 94.2 us
  Pallas kernels  91.9 us (97%)
  local copies, waits for them, and re-layouts  2.19 us (2%)
    pallas_call x1, Pallas kernels, local(): pl.pallas_call(functools.partial(exchange_kernel, n, m, groups), out_shap...  85.6 us
    pallas_call x1, Pallas kernels, local(): pl.pallas_call(norm_kernel, grid=(length // tile,), out_shape=jax.ShapeDt...  6.34 us
    unnamed x6, local copies, waits for them, and re-layouts  2.19 us

commit v1 on v0

v1 whole, which is shorter than its diff:
```python
import functools

import jax
import jax.numpy as jnp
from jax import lax
from jax.experimental import pallas as pl
from jax.experimental.pallas import tpu as pltpu
from jax.sharding import PartitionSpec as P

HEAD_DIM = 64
STATE = 128
BLOCK = 256
CHUNK = 256
SKEW = 3
TURN = 3
ROWS = 32
MESH = pl.DeviceIdType.MESH
F32 = jnp.float32
BF16 = jnp.bfloat16


def split_terms(value, terms):
    parts = []
    for _ in range(terms):
        part = value.astype(BF16)
        parts.append(part)
        value = value - part.astype(F32)
    return parts


def widen(table, ref):
    lane = lax.broadcasted_iota(jnp.int32, (table.shape[0], 128), 1)
    per_tile = 128 // HEAD_DIM
    for j in range(ref.shape[1] // 128):
        tile = jnp.broadcast_to(table[:, j * per_tile : j * per_tile + 1], lane.shape)
        for i in range(1, per_tile):
            column = j * per_tile + i
            tile = jnp.where(lane >= i * HEAD_DIM, jnp.broadcast_to(table[:, column : column + 1], lane.shape), tile)
        ref[:, j * 128 : (j + 1) * 128] = tile


def exchange_kernel(
    n, m, groups,
    x_hbm, gate_hbm, b_hbm, c_hbm, logit_hbm, bias_hbm, decay_hbm, skip_hbm, starts_hbm,
    gated_ref, power_ref,
    x_ref, gate_ref, b_ref, c_ref, logit_ref, bias_ref, decay_ref, skip_ref, starts_ref,
    keys_ref, scores_ref, spread_ref, param_ref,
    tail_ref, up_ref, down_ref, out_ref, skips_ref, line_ref, coef_ref,
    own_ref, sum_ref, before_ref, inside_ref,
    step_send, step_recv, fore_send, fore_recv, back_send, back_recv,
    param_in, decay_out, decay_in, hop_out, hop_in,
    param_sems, decay_sems, hop_sems, step_sems, fore_sems, back_sems, load_sems,
):
    ci = lax.axis_index("ctx")
    zi = lax.axis_index("head")
    bits = m.bit_length() - 1
    length, inner = x_ref.shape
    heads = logit_ref.shape[1]
    count = inner // CHUNK
    per_group = count // groups
    chunk_heads = CHUNK // HEAD_DIM

    half = count // max(n, 4)
    first = 2 * half
    second = count - first
    z_turn = max(first, TURN + bits * SKEW)
    c_turn = max(TURN + second, (n - 1) * SKEW)

    def first_chunk(i):
        return jnp.where(i < half, i, count - first + i)

    def second_chunk(i):
        return half + i

    pairs = (
        (bias_hbm, bias_ref), (decay_hbm, decay_ref), (skip_hbm, skip_ref), (starts_hbm, starts_ref),
        (b_hbm, b_ref), (c_hbm, c_ref), (logit_hbm, logit_ref), (x_hbm, x_ref), (gate_hbm, gate_ref),
    )
    loads = [pltpu.make_async_copy(src, dst, load_sems.at[i]) for i, (src, dst) in enumerate(pairs)]
    for load in loads:
        load.start()

    def z_peer(d):
        return (ci, lax.rem(zi + d, n))

    def ctx_peer(d):
        return (lax.rem(ci + d, m), zi)

    def ctx_partner(j):
        bit = 1 << j
        upper = lax.rem(ci // bit, 2)
        return ci + bit - 2 * bit * upper, upper

    barrier = pltpu.get_barrier_semaphore()
    for d in range(1, n):
        pl.semaphore_signal(barrier, inc=1, device_id=z_peer(d), device_id_type=MESH)
    for d in range(1, m):
        pl.semaphore_signal(barrier, inc=1, device_id=ctx_peer(d), device_id_type=MESH)

    own_heads = bias_ref.shape[1]
    place = jnp.where(
        lax.broadcasted_iota(jnp.int32, (own_heads, heads), 0) + zi * own_heads
        == lax.broadcasted_iota(jnp.int32, (own_heads, heads), 1), 1.0, 0.0
    ).astype(BF16)
    for load in loads[:4]:
        load.wait()
    raw = jnp.concatenate(
        [bias_ref[...], decay_ref[...], skip_ref[...], jnp.zeros((5, own_heads), F32)], axis=0
    )
    placed = jnp.zeros((8, heads), F32)
    for part in split_terms(raw, 3):
        placed = placed + jnp.dot(part, place, preferred_element_type=F32)
    param_ref[...] = placed

    def remote(src, dst, sems, index, device):
        return pltpu.make_async_remote_copy(
            src_ref=src, dst_ref=dst, send_sem=sems.at[(0, *index)], recv_sem=sems.at[(1, *index)],
            device_id=device, device_id_type=MESH,
        )

    param_copies = [
        remote(param_ref, param_in.at[d], param_sems, (d,), z_peer(d)) for d in range(1, n)
    ]
    decay_copies = [
        remote(decay_out, decay_in.at[d], decay_sems, (d,), z_peer(d)) for d in range(1, n)
    ]
    hop_copies = [
        remote(hop_out, hop_in.at[d], hop_sems, (d,), ctx_peer(d)) for d in range(1, m)
    ]
    pl.semaphore_wait(barrier, n - 1 + m - 1)
    for copy in param_copies:
        copy.start()

    row = lax.broadcasted_iota(jnp.int32, (2 * heads, CHUNK), 0)
    lane = lax.broadcasted_iota(jnp.int32, (2 * heads, CHUNK), 1)

    def fill(k, _):
        own = lane // HEAD_DIM + k * chunk_heads
        spread_ref[k] = jnp.where((row == own) | (row == own + heads), 1.0, 0.0).astype(BF16)
        return 0

    lax.fori_loop(0, count, fill, 0)

    offset = lax.rem(zi * length, BLOCK)
    starts = starts_ref[...].astype(F32)
    mine = lax.broadcasted_iota(jnp.int32, starts.shape, 1) == zi * length // BLOCK
    start = jnp.sum(jnp.where(mine, starts, 0.0), axis=1, keepdims=True) - offset.astype(F32)
    start = jnp.where((start < 0.0) | (start >= length), float(length), start)
    row = lax.broadcasted_iota(jnp.int32, (length, length), 0).astype(F32)
    col = lax.broadcasted_iota(jnp.int32, (length, length), 1).astype(F32)
    lower = jnp.where(row >= col, 1.0, 0.0)
    same = jnp.where(row >= start, 1.0, 0.0) == jnp.where(col >= start, 1.0, 0.0)
    allowed = jnp.where(same, lower, 0.0)
    for load in loads[4:7]:
        load.wait()
    for g in range(groups):
        part = slice(g * STATE, (g + 1) * STATE)
        scores = lax.dot_general(
            c_ref[:, part], b_ref[:, part], (((1,), (1,)), ((), ())), preferred_element_type=F32
        )
        scores_ref[g] = jnp.where(allowed > 0.0, scores, 0.0).astype(BF16)
        keys_ref[g] = b_ref[:, part].astype(F32).T.astype(BF16)
    power_ref[...] = jnp.zeros_like(power_ref)

    for copy in param_copies:
        copy.wait()
    params = param_ref[...]
    for d in range(1, n):
        params = params + param_in[d]

    logits = logit_ref[...].astype(F32) + params[0:1]
    step = jnp.maximum(logits, 0.0) + jnp.log1p(jnp.exp(-jnp.abs(logits)))
    rate = -jnp.exp(params[1:2]) * step
    lower = lower.astype(BF16)
    cum = jnp.zeros((length, heads), F32)
    for part in split_terms(rate, 3)[::-1]:
        cum = cum + jnp.dot(lower, part, preferred_element_type=F32)
    last = cum[length - 1 : length]
    middle = cum[length // 2 - 1 : length // 2]
    position = lax.broadcasted_iota(jnp.int32, (length, heads), 0).astype(F32)
    begins = start < length
    carried = jnp.where(begins, 0.0, jnp.exp(last))

    decay_out[...] = jnp.broadcast_to(carried, decay_out.shape)
    for copy in decay_copies:
        copy.start()
    keep = position >= jnp.where(begins, start, 0.0)
    tail = jnp.where(keep, jnp.exp(last - cum), 0.0) * step
    tail_ref[...] = jnp.concatenate(split_terms(tail, 2), axis=1)
    up_ref[...] = jnp.concatenate(split_terms(jnp.exp(cum - middle), 2), axis=1)
    down_ref[...] = jnp.concatenate(split_terms(jnp.exp(middle - cum) * step, 2), axis=1)
    out_ref[...] = jnp.concatenate(
        split_terms(jnp.where(position < start, jnp.exp(cum), 0.0), 2), axis=1
    )
    widen(jnp.broadcast_to(params[2:3], (8, heads)), skips_ref)
    loads[7].wait()
    loads[8].wait()

    def step_copy(j, k):
        return remote(step_send.at[j, k], step_recv.at[j, k], step_sems, (j, k), (ctx_partner(j)[0], zi))

    def fore_copy(k):
        return remote(fore_send.at[k], fore_recv.at[k], fore_sems, (k,), (ci, lax.rem(zi + 1, n)))

    def back_copy(k):
        return remote(back_send.at[k], back_recv.at[k], back_sems, (k,), (ci, lax.rem(zi + n - 1, n)))

    def channels(k):
        return pl.ds(pl.multiple_of(k * CHUNK, CHUNK), CHUNK)

    def states(k):
        return pl.ds(pl.multiple_of((k // per_group) * STATE, STATE), STATE)

    def line(k, slot):
        return line_ref[slot : slot + 1, channels(k)]

    def coef(k, slot):
        return coef_ref[slot : slot + 1, channels(k)]

    is_last_upper = ctx_partner(bits - 1)[1] == 1
    is_last_lower = ctx_partner(bits - 1)[1] == 0

    def write(k):
        weight = jnp.dot(tail_ref[...], spread_ref[k], preferred_element_type=F32)
        scaled = (x_ref[:, channels(k)].astype(F32) * weight).astype(BF16)
        written = jnp.dot(keys_ref[k // per_group], scaled, preferred_element_type=F32)
        own_ref[k] = written
        return written

    def enter(k, value):
        sum_ref[k] = value
        step_send[0, k] = value.astype(BF16)
        step_copy(0, k).start()

    def look(k):
        x = x_ref[:, channels(k)].astype(F32)
        down = jnp.dot(down_ref[...], spread_ref[k], preferred_element_type=F32)
        up = jnp.dot(up_ref[...], spread_ref[k], preferred_element_type=F32)
        inside = jnp.dot(scores_ref[k // per_group], (x * down).astype(BF16), preferred_element_type=F32)
        inside_ref[k] = up * inside + skips_ref[0:1, channels(k)] * x

    def finish(k, with_back):
        incoming = before_ref[k]
        if with_back:
            incoming = incoming + back_recv[k].astype(F32)
        frozen = (fore_recv[k].astype(F32) + line(k, 1) * incoming).astype(BF16)
        outside = jnp.dot(c_ref[:, states(k)], frozen, preferred_element_type=F32)
        weight = jnp.dot(out_ref[...], spread_ref[k], preferred_element_type=F32)
        gate = gate_ref[:, channels(k)].astype(F32)
        gated = (outside * weight + inside_ref[k]) * (gate / (1.0 + jnp.exp(-gate)))
        gated_ref[:, channels(k)] = gated.astype(BF16)
        square = gated * gated
        total = power_ref[...]
        for i in range(CHUNK // 128):
            total = total + square[:, i * 128 : (i + 1) * 128]
        power_ref[...] = total

    fore_at = zi * SKEW
    back_at = (n - 1 - zi) * SKEW
    done_at = jnp.maximum(fore_at, back_at)

    def iteration(t, _):
        @pl.when(t == TURN)
        def _():
            for copy in decay_copies:
                copy.wait()
            own = decay_out[...]
            before = jnp.ones((8, heads), F32)
            after = jnp.ones((8, heads), F32)
            for d in range(1, n):
                got = decay_in[d]
                before = before * jnp.where(zi >= d, got, 1.0)
                after = after * jnp.where(zi >= d, 1.0, got)
            hop_out[...] = before * own * after
            for copy in hop_copies:
                copy.start()
            widen(jnp.concatenate([own[0:1], before[0:1], after[0:1], own[3:8]], axis=0), line_ref)

        @pl.when(t == TURN + SKEW)
        def _():
            for copy in hop_copies:
                copy.wait()
            total = hop_out[...]
            ahead = jnp.ones((8, heads), F32)
            rows = []
            for j in range(bits):
                bit = 1 << j
                is_upper = ctx_partner(j)[1] == 1
                sibling = ctx_partner(j)[0] // bit
                got = jnp.ones((8, heads), F32)
                for d in range(1, m):
                    source = lax.rem(ci + m - d, m)
                    got = got * jnp.where(source // bit == sibling, hop_in[d], 1.0)
                rows.append(jnp.where(is_upper, 1.0, got))
                rows.append(jnp.where(is_upper, total, 1.0))
                rows.append(jnp.where(is_upper, ahead, 0.0))
                ahead = jnp.where(is_upper, ahead * got, ahead)
                total = total * got
            pad = [jnp.zeros((1, heads), F32)] * (coef_ref.shape[0] - len(rows))
            widen(jnp.concatenate([r[0:1] for r in rows] + pad, axis=0), coef_ref)

        @pl.when(t < first)
        def _():
            write(first_chunk(t))


        def fore(k, is_first):
            @pl.when(zi > 0)
            def _():
                fore_copy(k).wait_recv()

            @pl.when(zi == 0)
            def _():
                fore_recv[k] = jnp.zeros_like(fore_recv[k])
                if is_first:
                    fore_send[k] = own_ref[k].astype(BF16)
                    fore_copy(k).start()

            @pl.when((zi > 0) & (zi < n - 1) if is_first else zi < n - 1)
            def _():
                arrived = fore_recv[k].astype(F32)
                if not is_first:
                    arrived = arrived + line(k, 1) * before_ref[k]
                fore_send[k] = (line(k, 0) * arrived + own_ref[k]).astype(BF16)
                fore_copy(k).start()

        def back(k, is_first):
            @pl.when(zi < n - 1)
            def _():
                back_copy(k).wait_recv()

            @pl.when(zi == n - 1)
            def _():
                back_recv[k] = jnp.zeros_like(back_recv[k])
                if is_first:
                    back_send[k] = own_ref[k].astype(BF16)
                    back_copy(k).start()

            @pl.when((zi > 0) & (zi < n - 1) if is_first else zi > 0)
            def _():
                more = line(k, 2) * own_ref[k] if is_first else before_ref[k]
                back_send[k] = (back_recv[k].astype(F32) + more).astype(BF16)
                back_copy(k).start()

        for at, relay in ((fore_at, fore), (back_at, back)):
            s = t - at

            @pl.when((s >= 0) & (s < first))
            def _():
                relay(first_chunk(s), True)

            @pl.when((s >= z_turn) & (s < z_turn + second))
            def _():
                relay(second_chunk(s - z_turn), False)

        for j in range(bits):
            s = t - (j + 1) * SKEW
            is_second = (s >= TURN) & (s < TURN + second)
            is_first = (s >= c_turn) & (s < c_turn + first)

            @pl.when(is_second | is_first)
            def _(j=j, s=s):
                k = jnp.where(s < TURN + second, second_chunk(s - TURN), first_chunk(s - c_turn))

                def receive():
                    step_copy(j, k).wait_recv()
                    got = step_recv[j, k].astype(F32)
                    part = coef(k, 2 + 3 * j) * got
                    before_ref[k] = part if j == 0 else before_ref[k] + part
                    return got

                if j == bits - 1:
                    @pl.when(is_last_upper)
                    def _():
                        receive()

                else:
                    got = receive()
                    value = sum_ref[k] * coef(k, 3 * j) + coef(k, 1 + 3 * j) * got
                    sum_ref[k] = value

                    def send():
                        step_send[j + 1, k] = value.astype(BF16)
                        step_copy(j + 1, k).start()

                    if j == bits - 2:
                        pl.when(is_last_lower)(send)
                    else:
                        send()

        @pl.when((t >= TURN) & (t < TURN + second))
        def _():
            k = second_chunk(t - TURN)
            enter(k, line(k, 2) * write(k))

        @pl.when((t >= c_turn) & (t < c_turn + first))
        def _():
            k = first_chunk(t - c_turn)
            value = line(k, 0) * fore_recv[k].astype(F32) + own_ref[k]
            enter(k, line(k, 2) * value + back_recv[k].astype(F32))

        s = t - z_turn - done_at

        @pl.when((s >= 0) & (s < second))
        def _():
            finish(second_chunk(s), True)

        r = t - c_turn - bits * SKEW

        @pl.when((r >= 0) & (r < first))
        def _():
            finish(first_chunk(r), False)

        @pl.when(t < count)
        def _():
            look(t)

        return 0

    steps = max(z_turn + second + (n - 1) * SKEW, c_turn + first + bits * SKEW)
    lax.fori_loop(0, steps, iteration, 0)

    def drain(k, _):
        for j in range(bits - 1):
            step_copy(j, k).wait_send()

        @pl.when(is_last_lower)
        def _():
            step_copy(bits - 1, k).wait_send()

        @pl.when(zi < n - 1)
        def _():
            fore_copy(k).wait_send()

        @pl.when(zi > 0)
        def _():
            back_copy(k).wait_send()

        return 0

    lax.fori_loop(0, count, drain, 0)


def scale_kernel(gated_ref, power_ref, gain_ref, out_ref):
    inner = gated_ref.shape[1]
    power = jnp.sum(power_ref[...], axis=1, keepdims=True)
    factor = lax.rsqrt(power / inner + 1e-05)
    width = 1024
    for i in range(inner // width):
        part = slice(i * width, (i + 1) * width)
        out_ref[:, part] = (gated_ref[:, part].astype(F32) * factor * gain_ref[:, part]).astype(BF16)


def local(
    n, m,
    head_inputs, gate_inputs, write_keys, read_queries, step_logits,
    step_bias, decay_log, skip_scale, norm_gain, document_starts,
):
    length, inner = head_inputs.shape
    heads = step_logits.shape[1]
    groups = write_keys.shape[1] // STATE
    assert length <= BLOCK and BLOCK % length == 0 and m & (m - 1) == 0 and m > 2 and n > 1
    bits = m.bit_length() - 1
    count = inner // CHUNK
    coefs = -(-3 * bits // 8) * 8
    assert TURN <= SKEW and count % max(n, 4) == 0

    hbm = pl.BlockSpec(memory_space=pltpu.HBM)
    whole = pl.BlockSpec(memory_space=pltpu.VMEM)
    piece = (count, STATE, CHUNK)
    dma = pltpu.SemaphoreType.DMA
    gated, power = pl.pallas_call(
        functools.partial(exchange_kernel, n, m, groups),
        out_shape=(
            jax.ShapeDtypeStruct((length, inner), BF16),
            jax.ShapeDtypeStruct((length, 128), F32),
        ),
        in_specs=[hbm] * 9,
        out_specs=(whole, whole),
        scratch_shapes=[
            pltpu.VMEM((length, inner), BF16),
            pltpu.VMEM((length, inner), BF16),
            pltpu.VMEM(write_keys.shape, BF16),
            pltpu.VMEM(read_queries.shape, BF16),
            pltpu.VMEM(step_logits.shape, BF16),
            pltpu.VMEM((1, step_bias.shape[0]), F32),
            pltpu.VMEM((1, step_bias.shape[0]), F32),
            pltpu.VMEM((1, step_bias.shape[0]), F32),
            pltpu.VMEM((1, document_starts.shape[0]), jnp.int32),
            pltpu.VMEM((groups, STATE, length), BF16),
            pltpu.VMEM((groups, length, length), BF16),
            pltpu.VMEM((count, 2 * heads, CHUNK), BF16),
            pltpu.VMEM((8, heads), F32),
            pltpu.VMEM((length, 2 * heads), BF16),
            pltpu.VMEM((length, 2 * heads), BF16),
            pltpu.VMEM((length, 2 * heads), BF16),
            pltpu.VMEM((length, 2 * heads), BF16),
            pltpu.VMEM((8, inner), F32),
            pltpu.VMEM((8, inner), F32),
            pltpu.VMEM((coefs, inner), F32),
            pltpu.VMEM(piece, F32),
            pltpu.VMEM(piece, F32),
            pltpu.VMEM(piece, F32),
            pltpu.VMEM((count, length, CHUNK), F32),
            pltpu.VMEM((bits, *piece), BF16),
            pltpu.VMEM((bits, *piece), BF16),
            pltpu.VMEM(piece, BF16),
            pltpu.VMEM(piece, BF16),
            pltpu.VMEM(piece, BF16),
            pltpu.VMEM(piece, BF16),
            pltpu.VMEM((n, 8, heads), F32),
            pltpu.VMEM((8, heads), F32),
            pltpu.VMEM((n, 8, heads), F32),
            pltpu.VMEM((8, heads), F32),
            pltpu.VMEM((m, 8, heads), F32),
            dma((2, n)),
            dma((2, n)),
            dma((2, m)),
            dma((2, bits, count)),
            dma((2, count)),
            dma((2, count)),
            dma((9,)),
        ],
        compiler_params=pltpu.CompilerParams(
            collective_id=0, has_side_effects=True, vmem_limit_bytes=63 * 2**20
        ),
        name="exchange",
    )(
        head_inputs, gate_inputs, write_keys, read_queries, step_logits,
        step_bias[None], decay_log[None], skip_scale[None], document_starts[None],
    )

    tile = min(length, ROWS)
    return pl.pallas_call(
        scale_kernel,
        grid=(length // tile,),
        out_shape=jax.ShapeDtypeStruct((length, inner), BF16),
        in_specs=[
            pl.BlockSpec((tile, inner), lambda i: (i, 0)),
            pl.BlockSpec((tile, 128), lambda i: (i, 0)),
            pl.BlockSpec((1, inner), lambda i: (0, 0)),
        ],
        out_specs=pl.BlockSpec((tile, inner), lambda i: (i, 0)),
        compiler_params=pltpu.CompilerParams(vmem_limit_bytes=20 * 2**20),
        name="scale",
    )(gated, power, norm_gain[None])


def solution(mesh):
    tokens = P(("ctx", "head"), None)
    return jax.shard_map(
        functools.partial(local, mesh.shape["head"], mesh.shape["ctx"]),
        mesh=mesh,
        in_specs=(tokens,) * 5 + (P("head"), P("head"), P("head"), P(), P("ctx")),
        out_specs=tokens,
        check_vma=False,
    )
```

time: 94.3 us -> 80.6 us (0.85)
  Pallas kernels: 91.9 us -> 77.1 us
    pallas_call x1, Pallas kernels: 85.6 us -> 72.9 us  [local(): pl.pallas_call(functools.partial(exchange_kernel, n, m, groups), out_shap...]
    pallas_call x1, Pallas kernels: 6.34 us -> 4.19 us  [local(): pl.pallas_call(scale_kernel, grid=(length // tile,), out_shape=jax.ShapeD...]
where the time goes in v1:
time: 80.6 us; the launch traced here: 80.2 us
  Pallas kernels  77.1 us (96%)
  local copies, waits for them, and re-layouts  3.09 us (4%)
    pallas_call x1, Pallas kernels, local(): pl.pallas_call(functools.partial(exchange_kernel, n, m, groups), out_shap...  72.9 us
    pallas_call x1, Pallas kernels, local(): pl.pallas_call(scale_kernel, grid=(length // tile,), out_shape=jax.ShapeD...  4.19 us
    unnamed x6, local copies, waits for them, and re-layouts  3.09 us

profile of v1, /device:TPU:0, one launch (start us, length us, event | category | flops | bytes accessed | tf_op | source)
XLA Modules:
  0.0 80.2 jit_solution(5881401556250012027)
XLA Ops:
  0.0 0.0 copy-start.2
  0.0 72.9 %exchange.1 = (bf16[256,8192]{1,0:T(8,128)(2,1)}, f32[256,128]{1,0:T(8,128)}) custom-call(bf16[256,8192]{1,0:T(8,128)(2,1)} %x_hbm.1, bf16[256,8192]{1,0:T(8,128)(2,1)} %gate_hbm.1, bf16[256,1024]{1,0:T(8,128)(2,1)} %b_hbm.1, bf16[256,1024]{1,0:T(8,128)(2,1)} %c_hbm.1, bf16[256,128]{1,0:T(8,128)(2,1)} %logit_hbm.1, f32[1,32]{1,0:T(1,128)} %bitcast.6, ...), custom_call_target="tpu_custom_call" | custom-call | tf_op jit(solution)/shard_map/exchange/pallas_call | solution.py:472
  72.9 0.0 copy-done.2
  72.9 0.0 copy-start
  72.9 2.2 %copy-done = bf16[256,8192]{1,0:T(8,128)(2,1)S(1)} copy-done((bf16[256,8192]{1,0:T(8,128)(2,1)S(1)}, bf16[256,8192]{1,0:T(8,128)(2,1)}, u32[]{:S(2)}) %copy-start) | copy-done | bytes 4194328
  75.1 0.0 copy-start.1
  75.1 0.9 %copy-done.1 = f32[256,128]{1,0:T(8,128)S(1)} copy-done((f32[256,128]{1,0:T(8,128)S(1)}, f32[256,128]{1,0:T(8,128)}, u32[]{:S(2)}) %copy-start.1) | copy-done | bytes 131096
  76.0 4.2 %scale.1 = bf16[256,8192]{1,0:T(8,128)(2,1)} custom-call(bf16[256,8192]{1,0:T(8,128)(2,1)S(1)} %copy-done, f32[256,128]{1,0:T(8,128)S(1)} %copy-done.1, f32[1,8192]{1,0:T(1,128)S(1)} %bitcast.5), custom_call_target="tpu_custom_call" | custom-call | tf_op jit(solution)/shard_map/scale/pallas_call | solution.py:534
Async XLA Ops:
  0.0 72.9 %copy-start.2 = (f32[8192]{0:T(1024)S(1)}, f32[8192]{0:T(1024)}, u32[]{:S(2)}) copy-start(f32[8192]{0:T(1024)} %param.18) | copy-start | bytes 98308
  72.9 2.2 %copy-start = (bf16[256,8192]{1,0:T(8,128)(2,1)S(1)}, bf16[256,8192]{1,0:T(8,128)(2,1)}, u32[]{:S(2)}) copy-start(bf16[256,8192]{1,0:T(8,128)(2,1)} %get-tuple-element.7.gated_ref) | copy-start | bytes 12582916
  75.1 0.9 %copy-start.1 = (f32[256,128]{1,0:T(8,128)S(1)}, f32[256,128]{1,0:T(8,128)}, u32[]{:S(2)}) copy-start(f32[256,128]{1,0:T(8,128)} %get-tuple-element.8.power_ref) | copy-start | bytes 393220

commit v2 on v1

--- a/solution.py
+++ b/solution.py
@@ -49,7 +49,7 @@
     own_ref, sum_ref, before_ref, inside_ref,
     step_send, step_recv, fore_send, fore_recv, back_send, back_recv,
     param_in, decay_out, decay_in, hop_out, hop_in,
-    param_sems, decay_sems, hop_sems, step_sems, fore_sems, back_sems, load_sems,
+    param_sems, decay_sems, hop_sems, step_sems, relay_sems, fore_sems, back_sems, load_sems,
 ):
     ci = lax.axis_index("ctx")
     zi = lax.axis_index("head")
@@ -63,8 +63,10 @@
     half = count // max(n, 4)
     first = 2 * half
     second = count - first
-    z_turn = max(first, TURN + bits * SKEW)
-    c_turn = max(TURN + second, (n - 1) * SKEW)
+    z_turn = max(first, TURN + bits * SKEW + 1)
+    c_turn = (n - 1) * SKEW
+    c_done = c_turn + bits * SKEW + 1
+    assert c_done + half > count - half
 
     def first_chunk(i):
         return jnp.where(i < half, i, count - first + i)
@@ -199,6 +201,24 @@
     def step_copy(j, k):
         return remote(step_send.at[j, k], step_recv.at[j, k], step_sems, (j, k), (ctx_partner(j)[0], zi))
 
+    def relay_copy(j, k):
+        arrived = step_recv.at[j, k]
+        return remote(arrived, arrived, relay_sems, (j, k), (ctx_partner(0)[0], zi))
+
+    def is_mine(k):
+        return lax.rem(k, 2) == lax.rem(ci, 2)
+
+    def send(j, k, value):
+        def go():
+            sum_ref[k] = value
+            step_send[j, k] = value.astype(BF16)
+            step_copy(j, k).start()
+
+        if j == bits - 1:
+            pl.when(is_last_lower)(go)
+        else:
+            go()
+
     def fore_copy(k):
         return remote(fore_send.at[k], fore_recv.at[k], fore_sems, (k,), (ci, lax.rem(zi + 1, n)))
 
@@ -226,11 +246,6 @@
         written = jnp.dot(keys_ref[k // per_group], scaled, preferred_element_type=F32)
         own_ref[k] = written
         return written
-
-    def enter(k, value):
-        sum_ref[k] = value
-        step_send[0, k] = value.astype(BF16)
-        step_copy(0, k).start()
 
     def look(k):
         x = x_ref[:, channels(k)].astype(F32)
@@ -353,51 +368,57 @@
             def _():
                 relay(second_chunk(s - z_turn), False)
 
-        for j in range(bits):
-            s = t - (j + 1) * SKEW
-            is_second = (s >= TURN) & (s < TURN + second)
-            is_first = (s >= c_turn) & (s < c_turn + first)
-
-            @pl.when(is_second | is_first)
-            def _(j=j, s=s):
-                k = jnp.where(s < TURN + second, second_chunk(s - TURN), first_chunk(s - c_turn))
-
-                def receive():
-                    step_copy(j, k).wait_recv()
-                    got = step_recv[j, k].astype(F32)
-                    part = coef(k, 2 + 3 * j) * got
-                    before_ref[k] = part if j == 0 else before_ref[k] + part
-                    return got
-
+        def begin(k):
+            step_copy(0, k).wait_recv()
+            got = step_recv[0, k].astype(F32)
+            before_ref[k] = coef(k, 2) * got
+
+            @pl.when(is_mine(k))
+            def _():
+                send(1, k, sum_ref[k] * coef(k, 0) + coef(k, 1) * got)
+
+        def advance(j, k):
+            step_copy(j, k).wait_recv()
+            got = step_recv[j, k].astype(F32)
+
+            @pl.when(ctx_partner(j)[1] == 1)
+            def _():
+                relay_copy(j, k).start()
+                before_ref[k] += coef(k, 2 + 3 * j) * got
+
+            if j < bits - 1:
+                send(j + 1, k, sum_ref[k] * coef(k, 3 * j) + coef(k, 1 + 3 * j) * got)
+
+        def share(j, k):
+            relay_copy(j, k).wait_recv()
+            before_ref[k] += coef(k, 2 + 3 * j) * step_recv[j, k].astype(F32)
+
+        for begins_at, chunk, length_of in ((TURN, second_chunk, second), (c_turn, first_chunk, first)):
+            for j in range(bits):
+                s = t - begins_at - (j + 1) * SKEW
+                k = chunk(s)
+                inside = (s >= 0) & (s < length_of)
+                if j == 0:
+                    pl.when(inside)(functools.partial(begin, k))
+                    continue
                 if j == bits - 1:
-                    @pl.when(is_last_upper)
-                    def _():
-                        receive()
-
-                else:
-                    got = receive()
-                    value = sum_ref[k] * coef(k, 3 * j) + coef(k, 1 + 3 * j) * got
-                    sum_ref[k] = value
-
-                    def send():
-                        step_send[j + 1, k] = value.astype(BF16)
-                        step_copy(j + 1, k).start()
-
-                    if j == bits - 2:
-                        pl.when(is_last_lower)(send)
-                    else:
-                        send()
+                    inside = inside & is_last_upper
+                pl.when(inside & is_mine(k))(functools.partial(advance, j, k))
+                s = s - 1
+                k = chunk(s)
+                inside = (s >= 0) & (s < length_of) & (ctx_partner(j)[1] == 1)
+                pl.when(inside & jnp.logical_not(is_mine(k)))(functools.partial(share, j, k))
 
         @pl.when((t >= TURN) & (t < TURN + second))
         def _():
             k = second_chunk(t - TURN)
-            enter(k, line(k, 2) * write(k))
+            send(0, k, line(k, 2) * write(k))
 
         @pl.when((t >= c_turn) & (t < c_turn + first))
         def _():
             k = first_chunk(t - c_turn)
             value = line(k, 0) * fore_recv[k].astype(F32) + own_ref[k]
-            enter(k, line(k, 2) * value + back_recv[k].astype(F32))
+            send(0, k, line(k, 2) * value + back_recv[k].astype(F32))
 
         s = t - z_turn - done_at
 
@@ -405,7 +426,7 @@
         def _():
             finish(second_chunk(s), True)
 
-        r = t - c_turn - bits * SKEW
+        r = t - c_done
 
         @pl.when((r >= 0) & (r < first))
         def _():
@@ -417,16 +438,25 @@
 
         return 0
 
-    steps = max(z_turn + second + (n - 1) * SKEW, c_turn + first + bits * SKEW)
+    steps = max(z_turn + second + (n - 1) * SKEW, c_done + first)
     lax.fori_loop(0, steps, iteration, 0)
 
     def drain(k, _):
-        for j in range(bits - 1):
-            step_copy(j, k).wait_send()
-
-        @pl.when(is_last_lower)
-        def _():
-            step_copy(bits - 1, k).wait_send()
+        step_copy(0, k).wait_send()
+
+        @pl.when(is_mine(k))
+        def _():
+            for j in range(1, bits - 1):
+                step_copy(j, k).wait_send()
+
+            @pl.when(is_last_lower)
+            def _():
+                step_copy(bits - 1, k).wait_send()
+
+            for j in range(1, bits):
+                @pl.when(ctx_partner(j)[1] == 1)
+                def _(j=j):
+                    relay_copy(j, k).wait_send()
 
         @pl.when(zi < n - 1)
         def _():
@@ -441,14 +471,24 @@
     lax.fori_loop(0, count, drain, 0)
 
 
-def scale_kernel(gated_ref, power_ref, gain_ref, out_ref):
-    inner = gated_ref.shape[1]
-    power = jnp.sum(power_ref[...], axis=1, keepdims=True)
-    factor = lax.rsqrt(power / inner + 1e-05)
+def scale_kernel(gated_ref, power_ref, gain_ref, out_hbm, out_ref, sems):
+    length, inner = gated_ref.shape
+    tiles = sems.shape[0]
+    tile = length // tiles
     width = 1024
-    for i in range(inner // width):
-        part = slice(i * width, (i + 1) * width)
-        out_ref[:, part] = (gated_ref[:, part].astype(F32) * factor * gain_ref[:, part]).astype(BF16)
+    copies = []
+    for i in range(tiles):
+        rows = slice(i * tile, (i + 1) * tile)
+        power = jnp.sum(power_ref[rows], axis=1, keepdims=True)
+        factor = lax.rsqrt(power / inner + 1e-05)
+        for j in range(inner // width):
+            part = slice(j * width, (j + 1) * width)
+            out_ref[rows, part] = (gated_ref[rows, part].astype(F32) * factor * gain_ref[:, part]).astype(BF16)
+        copy = pltpu.make_async_copy(out_ref.at[rows], out_hbm.at[rows], sems.at[i])
+        copy.start()
+        copies.append(copy)
+    for copy in copies:
+        copy.wait()
 
 
 def local(
@@ -471,10 +511,7 @@
     dma = pltpu.SemaphoreType.DMA
     gated, power = pl.pallas_call(
         functools.partial(exchange_kernel, n, m, groups),
-        out_shape=(
-            jax.ShapeDtypeStruct((length, inner), BF16),
-            jax.ShapeDtypeStruct((length, 128), F32),
-        ),
+        out_shape=(pltpu.VMEM((length, inner), BF16), pltpu.VMEM((length, 128), F32)),
         in_specs=[hbm] * 9,
         out_specs=(whole, whole),
         scratch_shapes=[
@@ -517,12 +554,13 @@
             dma((2, n)),
             dma((2, m)),
             dma((2, bits, count)),
+            dma((2, bits, count)),
             dma((2, count)),
             dma((2, count)),
             dma((9,)),
         ],
         compiler_params=pltpu.CompilerParams(
-            collective_id=0, has_side_effects=True, vmem_limit_bytes=63 * 2**20
+            collective_id=0, has_side_effects=True, vmem_limit_bytes=58 * 2**20
         ),
         name="exchange",
     )(
@@ -530,17 +568,12 @@
         step_bias[None], decay_log[None], skip_scale[None], document_starts[None],
     )
 
-    tile = min(length, ROWS)
     return pl.pallas_call(
         scale_kernel,
-        grid=(length // tile,),
         out_shape=jax.ShapeDtypeStruct((length, inner), BF16),
-        in_specs=[
-            pl.BlockSpec((tile, inner), lambda i: (i, 0)),
-            pl.BlockSpec((tile, 128), lambda i: (i, 0)),
-            pl.BlockSpec((1, inner), lambda i: (0, 0)),
-        ],
-        out_specs=pl.BlockSpec((tile, inner), lambda i: (i, 0)),
+        in_specs=[whole] * 3,
+        out_specs=pl.BlockSpec(memory_space=pl.ANY),
+        scratch_shapes=[pltpu.VMEM((length, inner), BF16), dma((length // ROWS,))],
         compiler_params=pltpu.CompilerParams(vmem_limit_bytes=20 * 2**20),
         name="scale",
     )(gated, power, norm_gain[None])

time: 80.6 us -> 75.3 us (0.934)
  local copies, waits for them, and re-layouts: 3.09 us -> 0.01 us
  Pallas kernels: 77.1 us -> 75.1 us
    unnamed x6 -> x2, local copies, waits for them, and re-layouts: 3.09 us -> 0.01 us
    pallas_call x1, Pallas kernels: 4.19 us -> 2.27 us  [local(): pl.pallas_call(scale_kernel, out_shape=jax.ShapeDtypeStruct((length, inne...]
where the time goes in v2:
time: 75.3 us; the launch traced here: 75.1 us
  Pallas kernels  75.1 us (100%)
    pallas_call x1, Pallas kernels, local(): pl.pallas_call(functools.partial(exchange_kernel, n, m, groups), out_shap...  72.8 us
    pallas_call x1, Pallas kernels, local(): pl.pallas_call(scale_kernel, out_shape=jax.ShapeDtypeStruct((length, inne...  2.27 us

profile of v2, /device:TPU:0, one launch (start us, length us, event | category | flops | bytes accessed | tf_op | source)
XLA Modules:
  0.0 75.1 jit_solution(6258081874614560507)
XLA Ops:
  0.0 0.0 copy-start
  0.0 72.8 %exchange.1 = (bf16[256,8192]{1,0:T(8,128)(2,1)S(1)}, f32[256,128]{1,0:T(8,128)S(1)}) custom-call(bf16[256,8192]{1,0:T(8,128)(2,1)} %x_hbm.1, bf16[256,8192]{1,0:T(8,128)(2,1)} %gate_hbm.1, bf16[256,1024]{1,0:T(8,128)(2,1)} %b_hbm.1, bf16[256,1024]{1,0:T(8,128)(2,1)} %c_hbm.1, bf16[256,128]{1,0:T(8,128)(2,1)} %logit_hbm.1, f32[1,32]{1,0:T(1,128)} %bitcast.6, ...), custom_call_target="tpu_custom_call" | custom-call | tf_op jit(solution)/shard_map/exchange/pallas_call | solution.py:512
  72.8 0.0 copy-done
  72.8 2.3 %scale.1 = bf16[256,8192]{1,0:T(8,128)(2,1)} custom-call(bf16[256,8192]{1,0:T(8,128)(2,1)S(1)} %get-tuple-element.7.gated_ref, f32[256,128]{1,0:T(8,128)S(1)} %get-tuple-element.8.power_ref, f32[1,8192]{1,0:T(1,128)S(1)} %bitcast.5), custom_call_target="tpu_custom_call" | custom-call | tf_op jit(solution)/shard_map/scale/pallas_call | solution.py:571
Async XLA Ops:
  0.0 72.8 %copy-start = (f32[8192]{0:T(1024)S(1)}, f32[8192]{0:T(1024)}, u32[]{:S(2)}) copy-start(f32[8192]{0:T(1024)} %param.18) | copy-start | bytes 98308

commit v3 on v2

--- a/solution.py
+++ b/solution.py
@@ -12,7 +12,7 @@
 BLOCK = 256
 CHUNK = 256
 SKEW = 3
-TURN = 3
+TURN = 6
 ROWS = 32
 MESH = pl.DeviceIdType.MESH
 F32 = jnp.float32
@@ -41,15 +41,15 @@
 
 def exchange_kernel(
     n, m, groups,
-    x_hbm, gate_hbm, b_hbm, c_hbm, logit_hbm, bias_hbm, decay_hbm, skip_hbm, starts_hbm,
+    x_hbm, gate_hbm, gain_hbm, b_hbm, c_hbm, logit_hbm, bias_hbm, decay_hbm, skip_hbm, starts_hbm,
     gated_ref, power_ref,
-    x_ref, gate_ref, b_ref, c_ref, logit_ref, bias_ref, decay_ref, skip_ref, starts_ref,
+    x_ref, gate_ref, gain_ref, b_ref, c_ref, logit_ref, bias_ref, decay_ref, skip_ref, starts_ref,
     keys_ref, scores_ref, spread_ref, param_ref,
-    tail_ref, up_ref, down_ref, out_ref, skips_ref, line_ref, coef_ref,
+    tail_ref, up_ref, down_ref, out_ref, line_ref, coef_ref,
     own_ref, sum_ref, before_ref, inside_ref,
     step_send, step_recv, fore_send, fore_recv, back_send, back_recv,
     param_in, decay_out, decay_in, hop_out, hop_in,
-    param_sems, decay_sems, hop_sems, step_sems, relay_sems, fore_sems, back_sems, load_sems,
+    param_sems, decay_sems, hop_sems, step_sems, relay_sems, fore_sems, back_sems, sent_sems, load_sems,
 ):
     ci = lax.axis_index("ctx")
     zi = lax.axis_index("head")
@@ -63,10 +63,15 @@
     half = count // max(n, 4)
     first = 2 * half
     second = count - first
-    z_turn = max(first, TURN + bits * SKEW + 1)
-    c_turn = (n - 1) * SKEW
-    c_done = c_turn + bits * SKEW + 1
-    assert c_done + half > count - half
+    hops = [SKEW] + [SKEW * (j + 1) - 1 for j in range(1, bits)]
+    z_turn = max(first, TURN + hops[-1] + 2)
+    c_turn = half + (n - 1) * SKEW
+    c_done = c_turn + hops[-1] + 1
+    last_turn = max(z_turn + (n - 1) * SKEW, c_done)
+    look_turn = last_turn - count // 2
+    both = min(first, second)
+    assert look_turn > SKEW and count % 2 == 0
+    assert SKEW < TURN <= 2 * SKEW and TURN - SKEW <= half
 
     def first_chunk(i):
         return jnp.where(i < half, i, count - first + i)
@@ -77,9 +82,10 @@
     pairs = (
         (bias_hbm, bias_ref), (decay_hbm, decay_ref), (skip_hbm, skip_ref), (starts_hbm, starts_ref),
         (b_hbm, b_ref), (c_hbm, c_ref), (logit_hbm, logit_ref), (x_hbm, x_ref), (gate_hbm, gate_ref),
+        (gain_hbm, gain_ref),
     )
     loads = [pltpu.make_async_copy(src, dst, load_sems.at[i]) for i, (src, dst) in enumerate(pairs)]
-    for load in loads:
+    for load in loads[:-2]:
         load.start()
 
     def z_peer(d):
@@ -104,6 +110,34 @@
         lax.broadcasted_iota(jnp.int32, (own_heads, heads), 0) + zi * own_heads
         == lax.broadcasted_iota(jnp.int32, (own_heads, heads), 1), 1.0, 0.0
     ).astype(BF16)
+
+    def start_in_block():
+        offset = lax.rem(zi * length, BLOCK)
+        starts = starts_ref[...].astype(F32)
+        mine = lax.broadcasted_iota(jnp.int32, starts.shape, 1) == zi * length // BLOCK
+        start = jnp.sum(jnp.where(mine, starts, 0.0), axis=1, keepdims=True) - offset.astype(F32)
+        return jnp.where((start < 0.0) | (start >= length), float(length), start)
+
+    def decays(params):
+        logits = logit_ref[...].astype(F32) + params[0:1]
+        step = jnp.maximum(logits, 0.0) + jnp.log1p(jnp.exp(-jnp.abs(logits)))
+        rate = -jnp.exp(params[1:2]) * step
+        row = lax.broadcasted_iota(jnp.int32, (length, length), 0)
+        col = lax.broadcasted_iota(jnp.int32, (length, length), 1)
+        lower = jnp.where(row >= col, 1.0, 0.0).astype(BF16)
+        cum = jnp.zeros((length, heads), F32)
+        for part in split_terms(rate, 3)[::-1]:
+            cum = cum + jnp.dot(lower, part, preferred_element_type=F32)
+        last = cum[length - 1 : length]
+        position = lax.broadcasted_iota(jnp.int32, (length, heads), 0).astype(F32)
+        start = start_in_block()
+        begins = start < length
+        carried = jnp.where(begins, 0.0, jnp.exp(last))
+        keep = position >= jnp.where(begins, start, 0.0)
+        tail = jnp.where(keep, jnp.exp(last - cum), 0.0) * step
+        tail_ref[...] = jnp.concatenate(split_terms(tail, 2), axis=1)
+        return step, cum, carried, position, start
+
     for load in loads[:4]:
         load.wait()
     raw = jnp.concatenate(
@@ -112,11 +146,17 @@
     placed = jnp.zeros((8, heads), F32)
     for part in split_terms(raw, 3):
         placed = placed + jnp.dot(part, place, preferred_element_type=F32)
-    param_ref[...] = placed
-
-    def remote(src, dst, sems, index, device):
+    loads[6].wait()
+    early = decays(placed)[2]
+    owner = lax.broadcasted_iota(jnp.int32, (1, heads), 1) // own_heads == zi
+    param_ref[...] = jnp.concatenate(
+        [placed[0:3], jnp.where(owner, early, 0.0), placed[4:8]], axis=0
+    )
+
+    def remote(src, dst, sems, index, device, sent=None):
         return pltpu.make_async_remote_copy(
-            src_ref=src, dst_ref=dst, send_sem=sems.at[(0, *index)], recv_sem=sems.at[(1, *index)],
+            src_ref=src, dst_ref=dst, send_sem=sems.at[(0, *index)] if sent is None else sent_sems.at[sent],
+            recv_sem=sems.at[(1, *index)] if sent is None else sems.at[index],
             device_id=device, device_id_type=MESH,
         )
 
@@ -129,81 +169,78 @@
     hop_copies = [
         remote(hop_out, hop_in.at[d], hop_sems, (d,), ctx_peer(d)) for d in range(1, m)
     ]
+    row = lax.broadcasted_iota(jnp.int32, (heads, CHUNK), 0)
+    lane = lax.broadcasted_iota(jnp.int32, (heads, CHUNK), 1)
+
+    def fill(k, _):
+        spread = jnp.where(row == lane // HEAD_DIM + k * chunk_heads, 1.0, 0.0).astype(BF16)
+        spread_ref[k, :heads] = spread
+        spread_ref[k, heads:] = spread
+        return 0
+
+    def turn_keys(g):
+        keys_ref[g] = b_ref[:, g * STATE : (g + 1) * STATE].astype(F32).T.astype(BF16)
+
+    bases = (0, count - half)
+    soon = {k // per_group for base in bases for k in range(base, base + SKEW)}
+    for base in bases:
+        lax.fori_loop(base, base + SKEW, fill, 0)
+    loads[4].wait()
+    for g in sorted(soon):
+        turn_keys(g)
+    power_ref[...] = jnp.zeros_like(power_ref)
     pl.semaphore_wait(barrier, n - 1 + m - 1)
     for copy in param_copies:
         copy.start()
-
-    row = lax.broadcasted_iota(jnp.int32, (2 * heads, CHUNK), 0)
-    lane = lax.broadcasted_iota(jnp.int32, (2 * heads, CHUNK), 1)
-
-    def fill(k, _):
-        own = lane // HEAD_DIM + k * chunk_heads
-        spread_ref[k] = jnp.where((row == own) | (row == own + heads), 1.0, 0.0).astype(BF16)
-        return 0
-
-    lax.fori_loop(0, count, fill, 0)
-
-    offset = lax.rem(zi * length, BLOCK)
-    starts = starts_ref[...].astype(F32)
-    mine = lax.broadcasted_iota(jnp.int32, starts.shape, 1) == zi * length // BLOCK
-    start = jnp.sum(jnp.where(mine, starts, 0.0), axis=1, keepdims=True) - offset.astype(F32)
-    start = jnp.where((start < 0.0) | (start >= length), float(length), start)
-    row = lax.broadcasted_iota(jnp.int32, (length, length), 0).astype(F32)
-    col = lax.broadcasted_iota(jnp.int32, (length, length), 1).astype(F32)
-    lower = jnp.where(row >= col, 1.0, 0.0)
-    same = jnp.where(row >= start, 1.0, 0.0) == jnp.where(col >= start, 1.0, 0.0)
-    allowed = jnp.where(same, lower, 0.0)
-    for load in loads[4:7]:
-        load.wait()
-    for g in range(groups):
-        part = slice(g * STATE, (g + 1) * STATE)
-        scores = lax.dot_general(
-            c_ref[:, part], b_ref[:, part], (((1,), (1,)), ((), ())), preferred_element_type=F32
+    for load in loads[-2:]:
+        load.start()
+    loads[7].wait()
+
+    def settle():
+        lax.fori_loop(0, count, fill, 0)
+        for g in range(groups):
+            if g not in soon:
+                turn_keys(g)
+        start = start_in_block()
+        row = lax.broadcasted_iota(jnp.int32, (length, length), 0).astype(F32)
+        col = lax.broadcasted_iota(jnp.int32, (length, length), 1).astype(F32)
+        lower = jnp.where(row >= col, 1.0, 0.0)
+        same = jnp.where(row >= start, 1.0, 0.0) == jnp.where(col >= start, 1.0, 0.0)
+        allowed = jnp.where(same, lower, 0.0)
+        loads[5].wait()
+        for g in range(groups):
+            part = slice(g * STATE, (g + 1) * STATE)
+            scores = lax.dot_general(
+                c_ref[:, part], b_ref[:, part], (((1,), (1,)), ((), ())), preferred_element_type=F32
+            )
+            scores_ref[g] = jnp.where(allowed > 0.0, scores, 0.0).astype(BF16)
+
+        for copy in param_copies:
+            copy.wait()
+        params = param_ref[...]
+        for d in range(1, n):
+            params = params + param_in[d]
+        step, cum, carried, position, start = decays(params)
+        decay_out[...] = jnp.broadcast_to(carried, decay_out.shape)
+        for copy in decay_copies:
+            copy.start()
+        middle = cum[length // 2 - 1 : length // 2]
+        up_ref[...] = jnp.concatenate(split_terms(jnp.exp(cum - middle), 2), axis=1)
+        down_ref[...] = jnp.concatenate(split_terms(jnp.exp(middle - cum) * step, 2), axis=1)
+        out_ref[...] = jnp.concatenate(
+            split_terms(jnp.where(position < start, jnp.exp(cum), 0.0), 2), axis=1
         )
-        scores_ref[g] = jnp.where(allowed > 0.0, scores, 0.0).astype(BF16)
-        keys_ref[g] = b_ref[:, part].astype(F32).T.astype(BF16)
-    power_ref[...] = jnp.zeros_like(power_ref)
-
-    for copy in param_copies:
-        copy.wait()
-    params = param_ref[...]
-    for d in range(1, n):
-        params = params + param_in[d]
-
-    logits = logit_ref[...].astype(F32) + params[0:1]
-    step = jnp.maximum(logits, 0.0) + jnp.log1p(jnp.exp(-jnp.abs(logits)))
-    rate = -jnp.exp(params[1:2]) * step
-    lower = lower.astype(BF16)
-    cum = jnp.zeros((length, heads), F32)
-    for part in split_terms(rate, 3)[::-1]:
-        cum = cum + jnp.dot(lower, part, preferred_element_type=F32)
-    last = cum[length - 1 : length]
-    middle = cum[length // 2 - 1 : length // 2]
-    position = lax.broadcasted_iota(jnp.int32, (length, heads), 0).astype(F32)
-    begins = start < length
-    carried = jnp.where(begins, 0.0, jnp.exp(last))
-
-    decay_out[...] = jnp.broadcast_to(carried, decay_out.shape)
-    for copy in decay_copies:
-        copy.start()
-    keep = position >= jnp.where(begins, start, 0.0)
-    tail = jnp.where(keep, jnp.exp(last - cum), 0.0) * step
-    tail_ref[...] = jnp.concatenate(split_terms(tail, 2), axis=1)
-    up_ref[...] = jnp.concatenate(split_terms(jnp.exp(cum - middle), 2), axis=1)
-    down_ref[...] = jnp.concatenate(split_terms(jnp.exp(middle - cum) * step, 2), axis=1)
-    out_ref[...] = jnp.concatenate(
-        split_terms(jnp.where(position < start, jnp.exp(cum), 0.0), 2), axis=1
-    )
-    widen(jnp.broadcast_to(params[2:3], (8, heads)), skips_ref)
-    loads[7].wait()
-    loads[8].wait()
+        rest = jnp.zeros((4, heads), F32)
+        widen(jnp.concatenate([carried, carried, params[3:4], params[2:3], rest], axis=0), line_ref)
+        loads[8].wait()
+        loads[9].wait()
 
     def step_copy(j, k):
-        return remote(step_send.at[j, k], step_recv.at[j, k], step_sems, (j, k), (ctx_partner(j)[0], zi))
+        return remote(step_send.at[j, k], step_recv.at[j, k], step_sems, (j, k), (ctx_partner(j)[0], zi), j)
 
     def relay_copy(j, k):
         arrived = step_recv.at[j, k]
-        return remote(arrived, arrived, relay_sems, (j, k), (ctx_partner(0)[0], zi))
+        return remote(arrived, arrived, relay_sems, (j, k), (ctx_partner(0)[0], zi), bits + j)
 
     def is_mine(k):
         return lax.rem(k, 2) == lax.rem(ci, 2)
@@ -220,10 +257,10 @@
             go()
 
     def fore_copy(k):
-        return remote(fore_send.at[k], fore_recv.at[k], fore_sems, (k,), (ci, lax.rem(zi + 1, n)))
+        return remote(fore_send.at[k], fore_recv.at[k], fore_sems, (k,), (ci, lax.rem(zi + 1, n)), 2 * bits)
 
     def back_copy(k):
-        return remote(back_send.at[k], back_recv.at[k], back_sems, (k,), (ci, lax.rem(zi + n - 1, n)))
+        return remote(back_send.at[k], back_recv.at[k], back_sems, (k,), (ci, lax.rem(zi + n - 1, n)), 2 * bits + 1)
 
     def channels(k):
         return pl.ds(pl.multiple_of(k * CHUNK, CHUNK), CHUNK)
@@ -247,34 +284,45 @@
         own_ref[k] = written
         return written
 
-    def look(k):
-        x = x_ref[:, channels(k)].astype(F32)
-        down = jnp.dot(down_ref[...], spread_ref[k], preferred_element_type=F32)
-        up = jnp.dot(up_ref[...], spread_ref[k], preferred_element_type=F32)
-        inside = jnp.dot(scores_ref[k // per_group], (x * down).astype(BF16), preferred_element_type=F32)
-        inside_ref[k] = up * inside + skips_ref[0:1, channels(k)] * x
-
-    def finish(k, with_back):
-        incoming = before_ref[k]
-        if with_back:
-            incoming = incoming + back_recv[k].astype(F32)
-        frozen = (fore_recv[k].astype(F32) + line(k, 1) * incoming).astype(BF16)
-        outside = jnp.dot(c_ref[:, states(k)], frozen, preferred_element_type=F32)
-        weight = jnp.dot(out_ref[...], spread_ref[k], preferred_element_type=F32)
-        gate = gate_ref[:, channels(k)].astype(F32)
-        gated = (outside * weight + inside_ref[k]) * (gate / (1.0 + jnp.exp(-gate)))
-        gated_ref[:, channels(k)] = gated.astype(BF16)
-        square = gated * gated
-        total = power_ref[...]
-        for i in range(CHUNK // 128):
-            total = total + square[:, i * 128 : (i + 1) * 128]
-        power_ref[...] = total
+    def look(*chunks):
+        inputs = [x_ref[:, channels(k)].astype(F32) for k in chunks]
+        downs = [jnp.dot(down_ref[...], spread_ref[k], preferred_element_type=F32) for k in chunks]
+        pulled = [(x * down).astype(BF16) for x, down in zip(inputs, downs)]
+        ups = [jnp.dot(up_ref[...], spread_ref[k], preferred_element_type=F32) for k in chunks]
+        insides = [
+            jnp.dot(scores_ref[k // per_group], p, preferred_element_type=F32)
+            for k, p in zip(chunks, pulled)
+        ]
+        for k, x, up, inside in zip(chunks, inputs, ups, insides):
+            inside_ref[k] = up * inside + line(k, 3) * x
+
+    def finish(*pairs):
+        frozens = []
+        for k, with_back in pairs:
+            incoming = before_ref[k]
+            if with_back:
+                incoming = incoming + back_recv[k].astype(F32)
+            frozens.append((fore_recv[k].astype(F32) + line(k, 1) * incoming).astype(BF16))
+        for (k, _), frozen in zip(pairs, frozens):
+            weight = jnp.dot(out_ref[...], spread_ref[k], preferred_element_type=F32)
+            outside = jnp.dot(c_ref[:, states(k)], frozen, preferred_element_type=F32)
+            half_gate = 0.5 * gate_ref[:, channels(k)].astype(F32)
+            gated = (outside * weight + inside_ref[k]) * (half_gate * (1.0 + jnp.tanh(half_gate)))
+            gated_ref[:, channels(k)] = (gated * gain_ref[:, channels(k)]).astype(BF16)
+            square = gated * gated
+            total = power_ref[...]
+            for i in range(CHUNK // 128):
+                total = total + square[:, i * 128 : (i + 1) * 128]
+            power_ref[...] = total
 
     fore_at = zi * SKEW
     back_at = (n - 1 - zi) * SKEW
-    done_at = jnp.maximum(fore_at, back_at)
+    head_at = jnp.minimum(fore_at, back_at + half)
+    rear_at = jnp.minimum(back_at, fore_at + half)
 
     def iteration(t, _):
+        pl.when(t == SKEW)(settle)
+
         @pl.when(t == TURN)
         def _():
             for copy in decay_copies:
@@ -289,9 +337,12 @@
             hop_out[...] = before * own * after
             for copy in hop_copies:
                 copy.start()
-            widen(jnp.concatenate([own[0:1], before[0:1], after[0:1], own[3:8]], axis=0), line_ref)
-
-        @pl.when(t == TURN + SKEW)
+            skip = param_ref[2:3]
+            for d in range(1, n):
+                skip = skip + param_in[d, 2:3]
+            widen(jnp.concatenate([own[0:1], before[0:1], after[0:1], skip, own[4:8]], axis=0), line_ref)
+
+        @pl.when(t == TURN + hops[0])
         def _():
             for copy in hop_copies:
                 copy.wait()
@@ -314,9 +365,10 @@
             pad = [jnp.zeros((1, heads), F32)] * (coef_ref.shape[0] - len(rows))
             widen(jnp.concatenate([r[0:1] for r in rows] + pad, axis=0), coef_ref)
 
-        @pl.when(t < first)
-        def _():
-            write(first_chunk(t))
+        for at, base in ((head_at, 0), (rear_at, count - half)):
+            @pl.when((t >= at) & (t < at + half))
+            def _(at=at, base=base):
+                write(base + t - at)
 
 
         def fore(k, is_first):
@@ -357,12 +409,12 @@
                 back_send[k] = (back_recv[k].astype(F32) + more).astype(BF16)
                 back_copy(k).start()
 
-        for at, relay in ((fore_at, fore), (back_at, back)):
+        for at, relay, turned in ((fore_at, fore, 0), (back_at, back, half)):
             s = t - at
 
             @pl.when((s >= 0) & (s < first))
             def _():
-                relay(first_chunk(s), True)
+                relay(first_chunk(lax.rem(s + turned, first)), True)
 
             @pl.when((s >= z_turn) & (s < z_turn + second))
             def _():
@@ -395,7 +447,7 @@
 
         for begins_at, chunk, length_of in ((TURN, second_chunk, second), (c_turn, first_chunk, first)):
             for j in range(bits):
-                s = t - begins_at - (j + 1) * SKEW
+                s = t - begins_at - hops[j]
                 k = chunk(s)
                 inside = (s >= 0) & (s < length_of)
                 if j == 0:
@@ -420,58 +472,61 @@
             value = line(k, 0) * fore_recv[k].astype(F32) + own_ref[k]
             send(0, k, line(k, 2) * value + back_recv[k].astype(F32))
 
-        s = t - z_turn - done_at
-
-        @pl.when((s >= 0) & (s < second))
+        s = t - last_turn
+
+        @pl.when((s >= 0) & (s < both))
         def _():
-            finish(second_chunk(s), True)
-
-        r = t - c_done
-
-        @pl.when((r >= 0) & (r < first))
+            finish((second_chunk(s), True), (first_chunk(s), False))
+
+        if second > both:
+            @pl.when((s >= both) & (s < second))
+            def _():
+                finish((second_chunk(s), True))
+
+        if first > both:
+            @pl.when((s >= both) & (s < first))
+            def _():
+                finish((first_chunk(s), False))
+
+        k = (t - look_turn) * 2
+
+        @pl.when((k >= 0) & (k < count))
         def _():
-            finish(first_chunk(r), False)
-
-        @pl.when(t < count)
-        def _():
-            look(t)
+            look(k, k + 1)
 
         return 0
 
-    steps = max(z_turn + second + (n - 1) * SKEW, c_done + first)
+    steps = last_turn + max(first, second)
     lax.fori_loop(0, steps, iteration, 0)
 
-    def drain(k, _):
-        step_copy(0, k).wait_send()
-
-        @pl.when(is_mine(k))
-        def _():
-            for j in range(1, bits - 1):
-                step_copy(j, k).wait_send()
-
-            @pl.when(is_last_lower)
-            def _():
-                step_copy(bits - 1, k).wait_send()
-
-            for j in range(1, bits):
-                @pl.when(ctx_partner(j)[1] == 1)
-                def _(j=j):
-                    relay_copy(j, k).wait_send()
-
-        @pl.when(zi < n - 1)
-        def _():
-            fore_copy(k).wait_send()
-
-        @pl.when(zi > 0)
-        def _():
-            back_copy(k).wait_send()
-
-        return 0
-
-    lax.fori_loop(0, count, drain, 0)
-
-
-def scale_kernel(gated_ref, power_ref, gain_ref, out_hbm, out_ref, sems):
+    def drain(part, sent):
+        pltpu.make_async_copy(part, part, sent_sems.at[sent]).wait()
+
+    drain(step_send.at[0], 0)
+    for j in range(1, bits):
+        is_upper = ctx_partner(j)[1] == 1
+
+        @pl.when(is_upper)
+        def _(j=j):
+            drain(step_recv.at[j, : count // 2], bits + j)
+
+        if j < bits - 1:
+            drain(step_send.at[j, : count // 2], j)
+        else:
+            @pl.when(jnp.logical_not(is_upper))
+            def _(j=j):
+                drain(step_send.at[j, : count // 2], j)
+
+    @pl.when(zi < n - 1)
+    def _():
+        drain(fore_send, 2 * bits)
+
+    @pl.when(zi > 0)
+    def _():
+        drain(back_send, 2 * bits + 1)
+
+
+def scale_kernel(gated_ref, power_ref, out_hbm, out_ref, sems):
     length, inner = gated_ref.shape
     tiles = sems.shape[0]
     tile = length // tiles
@@ -483,7 +538,7 @@
         factor = lax.rsqrt(power / inner + 1e-05)
         for j in range(inner // width):
             part = slice(j * width, (j + 1) * width)
-            out_ref[rows, part] = (gated_ref[rows, part].astype(F32) * factor * gain_ref[:, part]).astype(BF16)
+            out_ref[rows, part] = (gated_ref[rows, part].astype(F32) * factor).astype(BF16)
         copy = pltpu.make_async_copy(out_ref.at[rows], out_hbm.at[rows], sems.at[i])
         copy.start()
         copies.append(copy)
@@ -503,7 +558,7 @@
     bits = m.bit_length() - 1
     count = inner // CHUNK
     coefs = -(-3 * bits // 8) * 8
-    assert TURN <= SKEW and count % max(n, 4) == 0
+    assert count % max(n, 4) == 0
 
     hbm = pl.BlockSpec(memory_space=pltpu.HBM)
     whole = pl.BlockSpec(memory_space=pltpu.VMEM)
@@ -512,11 +567,12 @@
     gated, power = pl.pallas_call(
         functools.partial(exchange_kernel, n, m, groups),
         out_shape=(pltpu.VMEM((length, inner), BF16), pltpu.VMEM((length, 128), F32)),
-        in_specs=[hbm] * 9,
+        in_specs=[hbm] * 10,
         out_specs=(whole, whole),
         scratch_shapes=[
             pltpu.VMEM((length, inner), BF16),
             pltpu.VMEM((length, inner), BF16),
+            pltpu.VMEM((1, inner), F32),
             pltpu.VMEM(write_keys.shape, BF16),
             pltpu.VMEM(read_queries.shape, BF16),
             pltpu.VMEM(step_logits.shape, BF16),
@@ -532,7 +588,6 @@
             pltpu.VMEM((length, 2 * heads), BF16),
             pltpu.VMEM((length, 2 * heads), BF16),
             pltpu.VMEM((length, 2 * heads), BF16),
-            pltpu.VMEM((8, inner), F32),
             pltpu.VMEM((8, inner), F32),
             pltpu.VMEM((coefs, inner), F32),
             pltpu.VMEM(piece, F32),
@@ -553,30 +608,31 @@
             dma((2, n)),
             dma((2, n)),
             dma((2, m)),
-            dma((2, bits, count)),
-            dma((2, bits, count)),
-            dma((2, count)),
-            dma((2, count)),
-            dma((9,)),
+            dma((bits, count)),
+            dma((bits, count)),
+            dma((count,)),
+            dma((count,)),
+            dma((2 * bits + 2,)),
+            dma((10,)),
         ],
         compiler_params=pltpu.CompilerParams(
             collective_id=0, has_side_effects=True, vmem_limit_bytes=58 * 2**20
         ),
         name="exchange",
     )(
-        head_inputs, gate_inputs, write_keys, read_queries, step_logits,
+        head_inputs, gate_inputs, norm_gain[None], write_keys, read_queries, step_logits,
         step_bias[None], decay_log[None], skip_scale[None], document_starts[None],
     )
 
     return pl.pallas_call(
         scale_kernel,
         out_shape=jax.ShapeDtypeStruct((length, inner), BF16),
-        in_specs=[whole] * 3,
+        in_specs=[whole] * 2,
         out_specs=pl.BlockSpec(memory_space=pl.ANY),
         scratch_shapes=[pltpu.VMEM((length, inner), BF16), dma((length // ROWS,))],
         compiler_params=pltpu.CompilerParams(vmem_limit_bytes=20 * 2**20),
         name="scale",
-    )(gated, power, norm_gain[None])
+    )(gated, power)
 
 
 def solution(mesh):

time: 75.3 us -> 70.8 us (0.940)
  Pallas kernels: 75.1 us -> 70.6 us
    pallas_call x1, Pallas kernels: 72.8 us -> 68.4 us  [local(): pl.pallas_call(functools.partial(exchange_kernel, n, m, groups), out_shap...]
where the time goes in v3:
time: 70.8 us; the launch traced here: 70.6 us
  Pallas kernels  70.6 us (100%)
    pallas_call x1, Pallas kernels, local(): pl.pallas_call(functools.partial(exchange_kernel, n, m, groups), out_shap...  68.4 us
    pallas_call x1, Pallas kernels, local(): pl.pallas_call(scale_kernel, out_shape=jax.ShapeDtypeStruct((length, inne...  2.24 us

profile of v3, /device:TPU:0, one launch (start us, length us, event | category | flops | bytes accessed | tf_op | source)
XLA Modules:
  0.0 70.6 jit_solution(9944729479582272025)
XLA Ops:
  0.0 68.4 %exchange.1 = (bf16[256,8192]{1,0:T(8,128)(2,1)S(1)}, f32[256,128]{1,0:T(8,128)S(1)}) custom-call(bf16[256,8192]{1,0:T(8,128)(2,1)} %x_hbm.1, bf16[256,8192]{1,0:T(8,128)(2,1)} %gate_hbm.1, f32[1,8192]{1,0:T(1,128)} %bitcast.5, bf16[256,1024]{1,0:T(8,128)(2,1)} %b_hbm.1, bf16[256,1024]{1,0:T(8,128)(2,1)} %c_hbm.1, bf16[256,128]{1,0:T(8,128)(2,1)} %logit_hbm.1, ...), custom_call_target="tpu_custom_call" | custom-call | tf_op jit(solution)/shard_map/exchange/pallas_call | solution.py:567
  68.4 2.2 %scale.1 = bf16[256,8192]{1,0:T(8,128)(2,1)} custom-call(bf16[256,8192]{1,0:T(8,128)(2,1)S(1)} %get-tuple-element.7.gated_ref, f32[256,128]{1,0:T(8,128)S(1)} %get-tuple-element.8.power_ref), custom_call_target="tpu_custom_call" | custom-call | tf_op jit(solution)/shard_map/scale/pallas_call | solution.py:627

commit v4 on v3

--- a/solution.py
+++ b/solution.py
@@ -13,6 +13,7 @@
 CHUNK = 256
 SKEW = 3
 TURN = 6
+LEAD = 9
 ROWS = 32
 MESH = pl.DeviceIdType.MESH
 F32 = jnp.float32
@@ -63,14 +64,14 @@
     half = count // max(n, 4)
     first = 2 * half
     second = count - first
-    hops = [SKEW] + [SKEW * (j + 1) - 1 for j in range(1, bits)]
+    hops = [SKEW * (j + 1) - 1 for j in range(bits)]
     z_turn = max(first, TURN + hops[-1] + 2)
     c_turn = half + (n - 1) * SKEW
     c_done = c_turn + hops[-1] + 1
     last_turn = max(z_turn + (n - 1) * SKEW, c_done)
-    look_turn = last_turn - count // 2
+    look_turn = last_turn - LEAD
     both = min(first, second)
-    assert look_turn > SKEW and count % 2 == 0
+    assert look_turn > SKEW
     assert SKEW < TURN <= 2 * SKEW and TURN - SKEW <= half
 
     def first_chunk(i):
@@ -488,11 +489,18 @@
             def _():
                 finish((first_chunk(s), False))
 
-        k = (t - look_turn) * 2
-
-        @pl.when((k >= 0) & (k < count))
+        s = t - look_turn
+
+        @pl.when((s >= 0) & (s < both))
         def _():
-            look(k, k + 1)
+            look(second_chunk(s), first_chunk(s))
+
+        if first != second:
+            rest = second_chunk if second > both else first_chunk
+
+            @pl.when((s >= both) & (s < max(first, second)))
+            def _():
+                look(rest(s))
 
         return 0
 

time: 70.8 us -> 69 us (0.975)
  Pallas kernels: 70.6 us -> 68.8 us
    pallas_call x1, Pallas kernels: 68.4 us -> 66.6 us  [local(): pl.pallas_call(functools.partial(exchange_kernel, n, m, groups), out_shap...]
where the time goes in v4:
time: 69 us; the launch traced here: 68.8 us
  Pallas kernels  68.8 us (100%)
    pallas_call x1, Pallas kernels, local(): pl.pallas_call(functools.partial(exchange_kernel, n, m, groups), out_shap...  66.6 us
    pallas_call x1, Pallas kernels, local(): pl.pallas_call(scale_kernel, out_shape=jax.ShapeDtypeStruct((length, inne...  2.24 us

profile of v4, /device:TPU:0, one launch (start us, length us, event | category | flops | bytes accessed | tf_op | source)
XLA Modules:
  0.0 68.8 jit_solution(8957725402579698343)
XLA Ops:
  0.0 66.6 %exchange.1 = (bf16[256,8192]{1,0:T(8,128)(2,1)S(1)}, f32[256,128]{1,0:T(8,128)S(1)}) custom-call(bf16[256,8192]{1,0:T(8,128)(2,1)} %x_hbm.1, bf16[256,8192]{1,0:T(8,128)(2,1)} %gate_hbm.1, f32[1,8192]{1,0:T(1,128)} %bitcast.5, bf16[256,1024]{1,0:T(8,128)(2,1)} %b_hbm.1, bf16[256,1024]{1,0:T(8,128)(2,1)} %c_hbm.1, bf16[256,128]{1,0:T(8,128)(2,1)} %logit_hbm.1, ...), custom_call_target="tpu_custom_call" | custom-call | tf_op jit(solution)/shard_map/exchange/pallas_call | solution.py:575
  66.6 2.2 %scale.1 = bf16[256,8192]{1,0:T(8,128)(2,1)} custom-call(bf16[256,8192]{1,0:T(8,128)(2,1)S(1)} %get-tuple-element.7.gated_ref, f32[256,128]{1,0:T(8,128)S(1)} %get-tuple-element.8.power_ref), custom_call_target="tpu_custom_call" | custom-call | tf_op jit(solution)/shard_map/scale/pallas_call | solution.py:635

commit v5 on v4

--- a/solution.py
+++ b/solution.py
@@ -65,10 +65,11 @@
     first = 2 * half
     second = count - first
     hops = [SKEW * (j + 1) - 1 for j in range(bits)]
+    fast = hops[:-1] + [hops[-1] - 1]
     z_turn = max(first, TURN + hops[-1] + 2)
     c_turn = half + (n - 1) * SKEW
-    c_done = c_turn + hops[-1] + 1
-    last_turn = max(z_turn + (n - 1) * SKEW, c_done)
+    c_done = c_turn + fast[-1] + 1
+    last_turn = max(z_turn + (n - 1) * SKEW, c_done) + 1
     look_turn = last_turn - LEAD
     both = min(first, second)
     assert look_turn > SKEW
@@ -324,6 +325,22 @@
     def iteration(t, _):
         pl.when(t == SKEW)(settle)
 
+        s = t - last_turn
+
+        @pl.when((s >= 0) & (s < both))
+        def _():
+            finish((second_chunk(s), True), (first_chunk(s), False))
+
+        if second > both:
+            @pl.when((s >= both) & (s < second))
+            def _():
+                finish((second_chunk(s), True))
+
+        if first > both:
+            @pl.when((s >= both) & (s < first))
+            def _():
+                finish((first_chunk(s), False))
+
         @pl.when(t == TURN)
         def _():
             for copy in decay_copies:
@@ -358,9 +375,10 @@
                 for d in range(1, m):
                     source = lax.rem(ci + m - d, m)
                     got = got * jnp.where(source // bit == sibling, hop_in[d], 1.0)
-                rows.append(jnp.where(is_upper, 1.0, got))
-                rows.append(jnp.where(is_upper, total, 1.0))
                 rows.append(jnp.where(is_upper, ahead, 0.0))
+                if j < bits - 1:
+                    rows.append(jnp.where(is_upper, 1.0, got))
+                    rows.append(jnp.where(is_upper, total, 1.0))
                 ahead = jnp.where(is_upper, ahead * got, ahead)
                 total = total * got
             pad = [jnp.zeros((1, heads), F32)] * (coef_ref.shape[0] - len(rows))
@@ -424,11 +442,11 @@
         def begin(k):
             step_copy(0, k).wait_recv()
             got = step_recv[0, k].astype(F32)
-            before_ref[k] = coef(k, 2) * got
+            before_ref[k] = coef(k, 0) * got
 
             @pl.when(is_mine(k))
             def _():
-                send(1, k, sum_ref[k] * coef(k, 0) + coef(k, 1) * got)
+                send(1, k, sum_ref[k] * coef(k, 1) + coef(k, 2) * got)
 
         def advance(j, k):
             step_copy(j, k).wait_recv()
@@ -437,18 +455,20 @@
             @pl.when(ctx_partner(j)[1] == 1)
             def _():
                 relay_copy(j, k).start()
-                before_ref[k] += coef(k, 2 + 3 * j) * got
+                before_ref[k] += coef(k, 3 * j) * got
 
             if j < bits - 1:
-                send(j + 1, k, sum_ref[k] * coef(k, 3 * j) + coef(k, 1 + 3 * j) * got)
+                send(j + 1, k, sum_ref[k] * coef(k, 1 + 3 * j) + coef(k, 2 + 3 * j) * got)
 
         def share(j, k):
             relay_copy(j, k).wait_recv()
-            before_ref[k] += coef(k, 2 + 3 * j) * step_recv[j, k].astype(F32)
-
-        for begins_at, chunk, length_of in ((TURN, second_chunk, second), (c_turn, first_chunk, first)):
+            before_ref[k] += coef(k, 3 * j) * step_recv[j, k].astype(F32)
+
+        for begins_at, chunk, length_of, after in (
+            (TURN, second_chunk, second, hops), (c_turn, first_chunk, first, fast),
+        ):
             for j in range(bits):
-                s = t - begins_at - hops[j]
+                s = t - begins_at - after[j]
                 k = chunk(s)
                 inside = (s >= 0) & (s < length_of)
                 if j == 0:
@@ -472,22 +492,6 @@
             k = first_chunk(t - c_turn)
             value = line(k, 0) * fore_recv[k].astype(F32) + own_ref[k]
             send(0, k, line(k, 2) * value + back_recv[k].astype(F32))
-
-        s = t - last_turn
-
-        @pl.when((s >= 0) & (s < both))
-        def _():
-            finish((second_chunk(s), True), (first_chunk(s), False))
-
-        if second > both:
-            @pl.when((s >= both) & (s < second))
-            def _():
-                finish((second_chunk(s), True))
-
-        if first > both:
-            @pl.when((s >= both) & (s < first))
-            def _():
-                finish((first_chunk(s), False))
 
         s = t - look_turn
 
@@ -565,7 +569,7 @@
     assert length <= BLOCK and BLOCK % length == 0 and m & (m - 1) == 0 and m > 2 and n > 1
     bits = m.bit_length() - 1
     count = inner // CHUNK
-    coefs = -(-3 * bits // 8) * 8
+    coefs = -(-(3 * bits - 2) // 8) * 8
     assert count % max(n, 4) == 0
 
     hbm = pl.BlockSpec(memory_space=pltpu.HBM)

time: 69 us -> 68.3 us (0.990)
  Pallas kernels: 68.8 us -> 68.1 us
where the time goes in v5:
time: 68.3 us; the launch traced here: 68.2 us
  Pallas kernels  68.1 us (100%)
    pallas_call x1, Pallas kernels, local(): pl.pallas_call(functools.partial(exchange_kernel, n, m, groups), out_shap...  65.9 us
    pallas_call x1, Pallas kernels, local(): pl.pallas_call(scale_kernel, out_shape=jax.ShapeDtypeStruct((length, inne...  2.24 us

profile of v5, /device:TPU:0, one launch (start us, length us, event | category | flops | bytes accessed | tf_op | source)
XLA Modules:
  0.0 68.2 jit_solution(1364905313343813333)
XLA Ops:
  0.0 65.9 %exchange.1 = (bf16[256,8192]{1,0:T(8,128)(2,1)S(1)}, f32[256,128]{1,0:T(8,128)S(1)}) custom-call(bf16[256,8192]{1,0:T(8,128)(2,1)} %x_hbm.1, bf16[256,8192]{1,0:T(8,128)(2,1)} %gate_hbm.1, f32[1,8192]{1,0:T(1,128)} %bitcast.5, bf16[256,1024]{1,0:T(8,128)(2,1)} %b_hbm.1, bf16[256,1024]{1,0:T(8,128)(2,1)} %c_hbm.1, bf16[256,128]{1,0:T(8,128)(2,1)} %logit_hbm.1, ...), custom_call_target="tpu_custom_call" | custom-call | tf_op jit(solution)/shard_map/exchange/pallas_call | solution.py:579
  65.9 2.2 %scale.1 = bf16[256,8192]{1,0:T(8,128)(2,1)} custom-call(bf16[256,8192]{1,0:T(8,128)(2,1)S(1)} %get-tuple-element.7.gated_ref, f32[256,128]{1,0:T(8,128)S(1)} %get-tuple-element.8.power_ref), custom_call_target="tpu_custom_call" | custom-call | tf_op jit(solution)/shard_map/scale/pallas_call | solution.py:639

commit v6 on v5

--- a/solution.py
+++ b/solution.py
@@ -464,6 +464,12 @@
             relay_copy(j, k).wait_recv()
             before_ref[k] += coef(k, 3 * j) * step_recv[j, k].astype(F32)
 
+        @pl.when((t >= c_turn) & (t < c_turn + first))
+        def _():
+            k = first_chunk(t - c_turn)
+            value = line(k, 0) * fore_recv[k].astype(F32) + own_ref[k]
+            send(0, k, line(k, 2) * value + back_recv[k].astype(F32))
+
         for begins_at, chunk, length_of, after in (
             (TURN, second_chunk, second, hops), (c_turn, first_chunk, first, fast),
         ):
@@ -486,12 +492,6 @@
         def _():
             k = second_chunk(t - TURN)
             send(0, k, line(k, 2) * write(k))
-
-        @pl.when((t >= c_turn) & (t < c_turn + first))
-        def _():
-            k = first_chunk(t - c_turn)
-            value = line(k, 0) * fore_recv[k].astype(F32) + own_ref[k]
-            send(0, k, line(k, 2) * value + back_recv[k].astype(F32))
 
         s = t - look_turn
 

time: 68.3 us -> 68.3 us (level)
  no operation moved by 1% of the time
where the time goes in v6:
time: 68.3 us; the launch traced here: 68.2 us
  Pallas kernels  68.1 us (100%)
    pallas_call x1, Pallas kernels, local(): pl.pallas_call(functools.partial(exchange_kernel, n, m, groups), out_shap...  65.9 us
    pallas_call x1, Pallas kernels, local(): pl.pallas_call(scale_kernel, out_shape=jax.ShapeDtypeStruct((length, inne...  2.24 us

profile of v6, /device:TPU:0, one launch (start us, length us, event | category | flops | bytes accessed | tf_op | source)
XLA Modules:
  0.0 68.2 jit_solution(1852029549640953234)
XLA Ops:
  0.0 65.9 %exchange.1 = (bf16[256,8192]{1,0:T(8,128)(2,1)S(1)}, f32[256,128]{1,0:T(8,128)S(1)}) custom-call(bf16[256,8192]{1,0:T(8,128)(2,1)} %x_hbm.1, bf16[256,8192]{1,0:T(8,128)(2,1)} %gate_hbm.1, f32[1,8192]{1,0:T(1,128)} %bitcast.5, bf16[256,1024]{1,0:T(8,128)(2,1)} %b_hbm.1, bf16[256,1024]{1,0:T(8,128)(2,1)} %c_hbm.1, bf16[256,128]{1,0:T(8,128)(2,1)} %logit_hbm.1, ...), custom_call_target="tpu_custom_call" | custom-call | tf_op jit(solution)/shard_map/exchange/pallas_call | solution.py:579
  65.9 2.2 %scale.1 = bf16[256,8192]{1,0:T(8,128)(2,1)} custom-call(bf16[256,8192]{1,0:T(8,128)(2,1)S(1)} %get-tuple-element.7.gated_ref, f32[256,128]{1,0:T(8,128)S(1)} %get-tuple-element.8.power_ref), custom_call_target="tpu_custom_call" | custom-call | tf_op jit(solution)/shard_map/scale/pallas_call | solution.py:639
